TPU v7x, 512 devices: a whole 4x8x8 slice. The times are simulated.
512 devices in a mesh: row: 8 (over z), col: 8 (over x, core), depth: 8 (over y).
Axes of the slice: x: 4, y: 8, z: 8, core: 2. Of those that a mesh axis runs over, the one named last changes fastest.
Arguments:
- x_matrix: bfloat16 [4608, 4608], P(('row', 'depth'), 'col'), may hold values from -0.09375 to 0.09375
- tangent: bfloat16 [4608, 4608], P(('row', 'depth'), 'col'), may hold values from -6 to 6
- fill_x: int32 [36, 36], replicated, may hold values from 0 to 1, as said below
- fill_t: int32 [36, 36], replicated, may hold values from 0 to 1, as said below
Outputs:
- tangent_next: float32 [4608, 4608], P(('row', 'depth'), 'col')
Inputs may be any that keep to these rules, and one draw needn't show every extreme that they name: `fill_x`: 1 where the block of X is filled, else 0; every diagonal block is filled. `fill_t`: 1 where the block of X' is filled, else 0; every diagonal block is filled.
All inputs are finite; a program needn't handle non-finite values.
Results may differ from a plain program's by a relative error of at most 0.00098.
Values may be sent and summed in bfloat16 or wider, within the bound.
A program may use at most 64 MiB of HBM per device.

v0:
```python
import jax
import jax.numpy as jnp
from jax import lax
from jax.sharding import PartitionSpec as P

BLOCK = 128


def block_mask(fill, row_start, col_start, rows, cols):
    count = fill.shape[0]
    blocks = lax.iota(jnp.int32, count)
    row_ids = (row_start + lax.iota(jnp.int32, rows)) // BLOCK
    col_ids = (col_start + lax.iota(jnp.int32, cols)) // BLOCK
    row_hot = (row_ids[:, None] == blocks[None, :]).astype(jnp.float32)
    col_hot = (blocks[:, None] == col_ids[None, :]).astype(jnp.float32)
    inner = jnp.dot(row_hot, fill.astype(jnp.float32), precision=lax.Precision.HIGHEST)
    return jnp.dot(inner, col_hot, precision=lax.Precision.HIGHEST)


def left_panels(stacked):
    count, rows, width = stacked.shape
    layers = lax.axis_size("depth")
    columns = lax.axis_size("col")
    tiled = jnp.tile(stacked, (1, 1, columns))
    received = lax.all_to_all(tiled, ("col", "depth"), split_axis=2, concat_axis=1, tiled=True)
    return received.reshape(count, columns, layers, rows, rows)


def right_panels(stacked):
    count, rows, width = stacked.shape
    grid_rows = lax.axis_size("row")
    received = lax.all_gather(stacked, "row", axis=1, tiled=True)
    return received.reshape(count, grid_rows, rows, width)


def partial_rows(left, right, count):
    out = jnp.einsum("cdij,cjk->dik", left, right, preferred_element_type=jnp.float32)
    return out.reshape(count, right.shape[2])


def layer_sum(term_fn, rows):
    return lax.psum_scatter(
        term_fn(jnp.int32(0), lax.axis_size("depth") * rows),
        "depth",
        scatter_dimension=0,
        tiled=True,
    )


def body(x_matrix, tangent, fill_x, fill_t):
    rows, width = x_matrix.shape
    layers = lax.axis_size("depth")
    row_start = (lax.axis_index("row") * layers + lax.axis_index("depth")) * rows
    col_start = lax.axis_index("col") * width
    masked_x = (
        x_matrix.astype(jnp.float32) * block_mask(fill_x, row_start, col_start, rows, width)
    ).astype(jnp.bfloat16)
    masked_t = (
        tangent.astype(jnp.float32) * block_mask(fill_t, row_start, col_start, rows, width)
    ).astype(jnp.bfloat16)
    paired = jnp.stack([masked_x, masked_t])
    lefts = left_panels(paired)
    rights = right_panels(paired)
    left_x = lefts[0]
    left_t = lefts[1]
    right_x = rights[0]
    right_t = rights[1]

    def first_terms(start, count):
        square_term = partial_rows(left_x, right_x, count)
        cross_term = partial_rows(left_t, right_x, count)
        return jnp.concatenate([square_term, cross_term], axis=1)

    firsts = layer_sum(first_terms, rows).astype(jnp.bfloat16)
    square = firsts[:, :width]
    cross = firsts[:, width:]
    left_square = left_panels(square[None])[0]
    seconds = right_panels(jnp.stack([square, cross]))
    right_square = seconds[0]
    right_cross = seconds[1]

    def last_terms(start, count):
        total = partial_rows(left_t, right_square, count)
        total = total + partial_rows(left_x, right_cross, count)
        return total + partial_rows(left_square, right_t, count)

    summed = layer_sum(last_terms, rows)
    return 1.5 * masked_t.astype(jnp.float32) - 0.5 * summed


def solution(mesh):
    placed = (P(("row", "depth"), "col"), P(("row", "depth"), "col"), P(), P())
    return jax.shard_map(
        body, mesh=mesh, in_specs=placed, out_specs=P(("row", "depth"), "col"), check_vma=False
    )
```

profile of v0, /device:TPU:6, one launch (start us, length us, event | category | flops | bytes accessed | tf_op | source)
XLA Modules:
  0.0 273.2 jit_solution(16946444617492353569)
XLA Ops:
  6.6 1.0 fusion.6
  7.5 1.0 fusion.5
  8.5 1.2 fusion
  9.7 1.2 fusion.2
  11.0 0.2 copy.24
  11.2 2.7 tile.8
  13.9 10.8 %all-to-all-start = ((bf16[2,72,4608]{1,0,2:T(2,128)(2,1)}), bf16[2,72,4608]{1,0,2:T(2,128)(2,1)S(1)}, u32[]{:S(2)}, u32[]{:S(2)}) async-start(bf16[2,72,4608]{1,0,2:T(2,128)(2,1)} %bitcast.67), calls=%async_computation | async-start | bytes 4718592 | tf_op jit(solution)/shard_map/all_to_all | solution.py:25
  24.7 0.0 all-gather.3.cloned.1.call-start
  24.8 0.7 all-gather.3.cloned.1.call-update
  25.5 49.1 %all-gather.3.cloned.1.call-done = bf16[2,576,576]{2,1,0:T(8,128)(2,1)} async-done(((bf16[2,72,576]{2,1,0:T(8,128)(2,1)}), bf16[2,576,576]{2,1,0:T(8,128)(2,1)}) %all-gather.3.cloned.1.call-update) | async-done | bytes 1327120 | tf_op jit(solution)/shard_map/all_gather | solution.py:32
  74.6 2.6 fusion.14
  77.2 1.8 all-to-all-done
  79.0 4.2 %copy.34 = bf16[2,72,64,72]{3,2,1,0:T(8,128)(2,1)} copy(bf16[2,72,64,72]{1,0,3,2:T(2,128)(2,1)S(1)} %bitcast.66) | data formatting | bytes 2654208 | tf_op jit(solution)/shard_map/all_to_all | solution.py:25
  83.2 2.1 slice_bitcast_fusion.1
  85.3 1.6 copy.27
  87.0 1.9 dot_general.44
  88.8 1.6 copy.29
  90.5 1.9 dot_general.46
  92.4 0.8 convolution_bitcast_fusion
  93.2 0.3 copy-done.7
  93.5 0.8 convolution_bitcast_fusion.1
  94.4 2.0 pad_maximum_fusion
  96.4 0.0 all-gather.5.cloned.1.call-start
  96.4 49.3 %reduce-scatter.7.cloned.1.call-done = f32[72,1152]{1,0:T(8,128)} async-done(((f32[576,1152]{1,0:T(8,128)}), f32[72,1152]{1,0:T(8,128)}) %reduce-scatter.7.cloned.1.call-update) | async-done | bytes 331792
  145.7 1.0 convert_element_type.35
  146.7 0.1 fusion.16
  146.8 0.7 pad_maximum_fusion.2
  147.6 0.2 reduce-scatter.9.cloned.1.call-start
  147.8 0.1 tile.19
  147.9 0.5 tile.20
  148.4 3.0 %copy.30 = bf16[1,72,4608]{1,0,2:T(2,128)(2,1)S(1)} copy(bf16[1,72,4608]{2,1,0:T(8,128)(2,1)S(1)} %tile.20) | data formatting | bytes 1327104 | tf_op jit(solution)/shard_map/tile | solution.py:24
  151.4 0.5 broadcast.83
  151.9 25.1 %reduce = bf16[4608,72]{1,0:T(8,128)(2,1)S(1)} reduce(bf16[4608,1,72]{2,1,0:T(2,128)(2,1)S(1)} %bitcast.69, bf16[]{:T(256)} %broadcast.83), dimensions={1}, to_apply=%bitcast.52.reduce_sub_computation | reduce | bytes 1327106
  176.9 2.5 reshape.82
  179.5 29.2 %all_to_all.30 = bf16[64,2,2592]{2,1,0:T(2,128)(2,1)S(1)} all-to-all(bf16[64,2,2592]{2,1,0:T(2,128)(2,1)S(1)} %reshape.82), channel_id=1, replica_groups=mesh['row'=8,'col'=8,'depth'=8] {'col','depth'}, dimensions={0} | all-to-all | bytes 1327104 | tf_op jit(solution)/shard_map/all_to_all | solution.py:25
  208.7 1.9 reshape.83
  210.6 2.6 copy.31
  213.1 2.6 all_to_all.26
  215.7 1.6 copy.33
  217.4 1.0 dot_general.52
  218.4 1.5 fusion.15
  220.0 0.9 fusion.17
  220.8 0.2 copy-done.8
  221.1 0.8 fusion.18
  221.9 0.3 copy-done.3
  222.2 2.1 bitcast_add_fusion
  224.3 40.8 %reduce-scatter.9.cloned.1.call-done = f32[72,576]{1,0:T(8,128)} async-done(((f32[576,576]{1,0:T(8,128)}), f32[72,576]{1,0:T(8,128)}) %reduce-scatter.9.cloned.1.call-update) | async-done | bytes 165904
  265.1 1.6 multiply_subtract_fusion
  (23 shorter events, 0.2 us)
Async XLA Ops:
  9.7 1.2 copy-start.1
  11.0 2.9 %copy-start = (bf16[2,72,576]{2,1,0:T(8,128)(2,1)}, bf16[2,72,576]{2,1,0:T(8,128)(2,1)S(1)}, u32[]{:S(2)}) copy-start(bf16[2,72,576]{2,1,0:T(8,128)(2,1)S(1)} %pad_maximum_fusion.1) | copy-start | bytes 497668
  13.9 65.1 %all-to-all-start = ((bf16[2,72,4608]{1,0,2:T(2,128)(2,1)}), bf16[2,72,4608]{1,0,2:T(2,128)(2,1)S(1)}, u32[]{:S(2)}, u32[]{:S(2)}) async-start(bf16[2,72,4608]{1,0,2:T(2,128)(2,1)} %bitcast.67), calls=%async_computation | async-start | bytes 4718592 | tf_op jit(solution)/shard_map/all_to_all | solution.py:25
  24.7 49.9 %all-gather.3.cloned.1.call-start = ((), (), s32[]{:S(2)}) async-start(), calls=%async_computation.4 | async-start | bytes 1658880 | tf_op jit(solution)/shard_map/all_gather | solution.py:32
  25.5 120.3 %reduce-scatter.7.cloned.1.call-start = ((), (), s32[]{:S(2)}) async-start(), calls=%async_computation.6 | async-start | bytes 2985984
  90.5 1.9 copy-start.4
  90.5 1.9 copy-start.5
  92.4 1.1 copy-start.7
  96.4 122.0 %all-gather.5.cloned.1.call-start = ((), (), s32[]{:S(2)}) async-start(), calls=%async_computation.5 | async-start | bytes 1658880 | tf_op jit(solution)/shard_map/all_gather | solution.py:32
  147.6 117.5 %reduce-scatter.9.cloned.1.call-start = ((), (), s32[]{:S(2)}) async-start(), calls=%async_computation.7 | async-start | bytes 1658880
  218.4 1.6 copy-start.6
  220.0 1.1 copy-start.8
  221.1 1.1 copy-start.3
  224.3 40.8 %copy-start.2 = (bf16[72,576]{1,0:T(8,128)(2,1)S(1)}, bf16[72,576]{1,0:T(8,128)(2,1)}, u32[]{:S(2)}) copy-start(bf16[72,576]{1,0:T(8,128)(2,1)} %copy-done.1) | copy-start | bytes 248836
Sparse Core Ops, SparseCore 0:
  27.6 46.9 all-gather.2
  96.5 49.1 reduce-scatter.6
  147.8 42.9 all-gather.4
  224.4 40.5 reduce-scatter.8
where the time goes:
time: 274 us; the launch traced here: 273 us
  waiting for transfers between devices  142 us (52%)
  local copies, waits for them, and re-layouts  37.5 us (14%)
  other arithmetic  30.4 us (11%)
  blocking collectives  29.2 us (11%)
  between operations  13.4 us (5%)
  starting transfers between devices  11.1 us (4%)
  matrix products  9.83 us (4%)
    unnamed x6, waiting for transfers between devices  90.8 us
    all_gather x2, waiting for transfers between devices, right_panels(): received = lax.all_gather(stacked, 'row', axis=1, tiled=True)  49.2 us
    all_to_all x1, blocking collectives, left_panels(): lax.all_to_all(tiled, ('col', 'depth'), split_axis=2, concat_axis=1, tile...  29.2 us
    unnamed x1, other arithmetic  25.1 us
    dot_general x7, local copies, waits for them, and re-layouts, partial_rows(): jnp.einsum('cdij,cjk->dik', left, right, preferred_element_type=jnp.float32)  11.7 us
    all_to_all x1, starting transfers between devices, left_panels(): lax.all_to_all(tiled, ('col', 'depth'), split_axis=2, concat_axis=1, tile...  10.8 us
    all_to_all x3, local copies, waits for them, and re-layouts, left_panels(): lax.all_to_all(tiled, ('col', 'depth'), split_axis=2, concat_axis=1, tile...  9.39 us
    another operation x4, local copies, waits for them, and re-layouts, left_panels(): tiled = jnp.tile(stacked, (1, 1, columns))  6.27 us
  transfers between devices with their start and end apart: 5, of which 4 were waited for; matrix products, arithmetic and copies ran while one was open for 15% of the time, Pallas kernels for 0%

commit v1 on v0

v1 whole, which is shorter than its diff:
```python
import functools

import jax
import jax.numpy as jnp
from jax import lax
from jax.experimental import pallas as pl
from jax.experimental.pallas import tpu as pltpu
from jax.sharding import PartitionSpec as P

BLOCK = 128
MESH = pl.DeviceIdType.MESH
F32 = jnp.float32
BF16 = jnp.bfloat16
N = 8
NX = 4
ROWS = 72
PAD = 80
WIDTH = 576
LANES = 640
HALVES = ((0, 256), (256, 320))


def kernel(
    x_ref, t_ref, fx_ref, ft_ref, out_ref,
    a1_send, a1_recv, lt, left, ra0, ra1, rb0, rb1,
    p_s0, p_d0, p_f0, p_s1, p_d1, p_f1,
    y_s0, y_d0, y_f0, y_s1, y_d1, y_f1, tm,
    a1_ss, a1_rs, z_ss, z_rs, y_ss, y_rs, x_ss, x_rs, c_ss, c_rs,
):
    r = lax.axis_index("row")
    c = lax.axis_index("col")
    d = lax.axis_index("depth")
    chip = c // 2
    core = lax.rem(c, 2)

    def wrap(value, size):
        return lax.rem(value + 2 * size, size)

    def at_row(step):
        return (wrap(r + step, N), c, d)

    def at_depth(step):
        return (r, c, wrap(d + step, N))

    def at_chip(step):
        return (r, wrap(chip + step, NX) * 2 + core, d)

    partner = (r, chip * 2 + 1 - core, d)

    barrier = pltpu.get_barrier_semaphore()
    greeted = [at_row(1), at_row(-1), at_chip(1), at_chip(-1), partner]
    greeted += [at_depth(s) for s in range(1, N)]
    for device in greeted:
        pl.semaphore_signal(barrier, inc=1, device_id=device, device_id_type=MESH)

    row_start = (r * N + d) * ROWS
    col_start = c * WIDTH

    def expand(fill):
        count = fill.shape[0]
        row_ids = (row_start + lax.broadcasted_iota(jnp.int32, (ROWS, count), 0)) >> 7
        row_hot = (row_ids == lax.broadcasted_iota(jnp.int32, (ROWS, count), 1)).astype(F32)
        col_ids = (col_start + lax.broadcasted_iota(jnp.int32, (count, WIDTH), 1)) >> 7
        col_hot = (col_ids == lax.broadcasted_iota(jnp.int32, (count, WIDTH), 0)).astype(F32)
        inner = jnp.dot(row_hot, fill.astype(F32), preferred_element_type=F32)
        return jnp.dot(inner, col_hot, preferred_element_type=F32)

    rights_a = (ra0, ra1)
    rights_b = (rb0, rb1)
    parts = ((p_s0, p_d0, p_f0), (p_s1, p_d1, p_f1))
    slots = ((y_s0, y_d0, y_f0), (y_s1, y_d1, y_f1))

    def chunk(index):
        return pl.ds(pl.multiple_of(index * PAD, 16), PAD)

    def block(index):
        return pl.ds(pl.multiple_of(index * ROWS, 8), ROWS)

    for m, (ref, fill) in enumerate(((x_ref, fx_ref), (t_ref, ft_ref))):
        masked = ref[...].astype(F32) * expand(fill[...])
        if m == 1:
            tm[...] = masked
        tall = jnp.concatenate([masked, jnp.zeros((PAD - ROWS, WIDTH), F32)], axis=0)
        for j in range(N):
            piece = tall[:, j * ROWS : (j + 1) * ROWS]
            wide = jnp.concatenate([piece, jnp.zeros((PAD, 128 - ROWS), F32)], axis=1)
            a1_send[m, j] = wide.astype(BF16)
        for h, (start, width) in enumerate(HALVES):
            rights_a[h][m, chunk(r), :] = tall[:, start : start + width].astype(BF16)
    for m in range(2):
        a1_recv[m, d] = a1_send[m, d]

    pl.semaphore_wait(barrier, len(greeted))

    sent = []

    def copy(src, dst, send_sem, recv_sem, device):
        return pltpu.make_async_remote_copy(
            src_ref=src, dst_ref=dst, send_sem=send_sem, recv_sem=recv_sem,
            device_id=device, device_id_type=MESH,
        )

    def send(src, dst, send_sem, recv_sem, device):
        made = copy(src, dst, send_sem, recv_sem, device)
        made.start()
        sent.append(made)

    def a1_start(m):
        for s in (4, 3, 5, 2, 6, 1, 7):
            to = wrap(d + s, N)
            send(a1_send.at[m, to], a1_recv.at[m, d], a1_ss.at[m, s], a1_rs.at[m, s], (r, c, to))

    def a1_finish(m):
        for s in range(1, N):
            came = wrap(d - s, N)
            slot = a1_recv.at[m, came]
            copy(slot, slot, a1_ss.at[m, s], a1_rs.at[m, s], partner).wait_recv()
        stacked = a1_recv[m].astype(F32)[:, :ROWS, :].reshape(N * ROWS, 128)
        turned = jnp.transpose(stacked)[:ROWS]
        turned = jnp.concatenate([turned, jnp.zeros((PAD - ROWS, WIDTH), F32)], axis=0)
        turned = jnp.concatenate([turned, jnp.zeros((PAD, LANES - WIDTH), F32)], axis=1)
        lt[m, chunk(c), :] = turned.astype(BF16)

    x_steps = ((2, 1), (1, 2))

    def lt_chunk(m, owner_chip, owner_core):
        return lt.at[m, chunk(owner_chip * 2 + owner_core), :]

    def core_send(m, k, owner_chip):
        piece = lt_chunk(m, owner_chip, core)
        send(piece, piece, c_ss.at[m, k], c_rs.at[m, k], partner)

    def x_step(m, s):
        if s == 0:
            core_send(m, 0, chip)
        for e, sign in enumerate((1, -1)):
            steps = x_steps[m][e]
            owner = wrap(chip - sign * s, NX)
            piece = lt_chunk(m, owner, core)
            if 0 < s <= steps:
                copy(piece, piece, x_ss.at[m, e, s - 1], x_rs.at[m, e, s - 1], partner).wait_recv()
            if s < steps:
                send(piece, piece, x_ss.at[m, e, s], x_rs.at[m, e, s], at_chip(sign))
            if 0 < s <= steps:
                core_send(m, 1 + e if s == 1 else 3, owner)

    def left_finish(m):
        long = 1 if x_steps[m][0] == 2 else -1
        for k, owner in enumerate((chip, chip - 1, chip + 1, chip - 2 * long)):
            piece = lt_chunk(m, wrap(owner, NX), 1 - core)
            copy(piece, piece, c_ss.at[m, k], c_rs.at[m, k], partner).wait_recv()
        for i in range(LANES // 128):
            lanes = slice(i * 128, (i + 1) * 128)
            left[m, lanes, :] = jnp.transpose(lt[m, :, lanes].astype(F32)).astype(BF16)

    ring_steps = ((4, 3), (3, 4))

    def z_step(stage, h, m, s):
        buf = (rights_a, rights_b)[stage][h]
        u = stage * 4 + h * 2 + m
        for e, sign in enumerate((1, -1)):
            steps = ring_steps[m][e]
            piece = buf.at[m, chunk(wrap(r - sign * s, N)), :]
            if 0 < s <= steps:
                copy(piece, piece, z_ss.at[u, e, s - 1], z_rs.at[u, e, s - 1], partner).wait_recv()
            if s < steps:
                send(piece, piece, z_ss.at[u, e, s], z_rs.at[u, e, s], at_row(sign))

    def y_step(h, k, s):
        part, slot = parts[h][k], slots[h][k]
        u = h * 3 + k
        for e, sign in enumerate((1, -1)):
            steps = ring_steps[(k + h) % 2][e]
            mine = part.at[block(wrap(d + sign * (steps - s), N)), :]
            if 0 < s <= steps:
                held = slot.at[e, s - 1]
                copy(held, held, y_ss.at[u, e, s - 1], y_rs.at[u, e, s - 1], partner).wait_recv()
                if s < steps:
                    slot[e, s - 1] = slot[e, s - 1] + mine[...]
            if s < steps:
                source = mine if s == 0 else slot.at[e, s - 1]
                send(source, slot.at[e, s], y_ss.at[u, e, s], y_rs.at[u, e, s], at_depth(sign))

    def y_total(h, k):
        part, slot = parts[h][k], slots[h][k]
        plus, minus = ring_steps[(k + h) % 2]
        return part[block(d), :] + slot[0, plus - 1] + slot[1, minus - 1]

    def multiply(out, terms):
        tile = 288

        def one(i, carry):
            rows = pl.ds(pl.multiple_of(i * tile, 16), tile)
            total = None
            for m, right in terms:
                term = jnp.dot(left[m, rows, :], right[...], preferred_element_type=F32)
                total = term if total is None else total + term
            out[rows, :] = total
            return carry

        lax.fori_loop(0, WIDTH // tile, one, 0)

    def firsts(h, k):
        right_x, right_t = rights_a[h].at[0], rights_a[h].at[1]
        if k == 0:
            multiply(parts[h][0], ((0, right_x),))
        else:
            multiply(parts[h][1], ((1, right_x), (0, right_t)))

    def second_start(h, k):
        total = y_total(h, k)
        tall = jnp.concatenate([total, jnp.zeros((PAD - ROWS, total.shape[1]), F32)], axis=0)
        rights_b[h][k, chunk(r), :] = tall.astype(BF16)
        z_step(1, h, k, 0)

    def seconds(h):
        multiply(parts[h][2], ((1, rights_b[h].at[0]), (0, rights_b[h].at[1])))

    def finish(h):
        start, width = HALVES[h]
        lanes = slice(start, start + width)
        out_ref[:, lanes] = 1.5 * tm[:, lanes] - 0.5 * y_total(h, 2)

    def z_all(stage, h, s):
        for m in range(2):
            z_step(stage, h, m, s)

    a1_start(0)
    z_all(0, 0, 0)
    a1_start(1)
    z_all(0, 1, 0)
    z_all(0, 0, 1)
    z_all(0, 1, 1)
    a1_finish(0)
    x_step(0, 0)
    z_all(0, 0, 2)
    a1_finish(1)
    x_step(1, 0)
    z_all(0, 1, 2)
    x_step(0, 1)
    z_all(0, 0, 3)
    x_step(0, 2)
    x_step(1, 1)
    z_step(0, 0, 0, 4)
    left_finish(0)
    firsts(0, 0)
    y_step(0, 0, 0)
    x_step(1, 2)
    z_all(0, 1, 3)
    z_step(0, 0, 1, 4)
    left_finish(1)
    firsts(0, 1)
    y_step(0, 1, 0)
    y_step(0, 0, 1)
    z_step(0, 1, 0, 4)
    firsts(1, 0)
    y_step(1, 0, 0)
    y_step(0, 1, 1)
    z_step(0, 1, 1, 4)
    firsts(1, 1)
    y_step(0, 0, 2)
    y_step(1, 1, 0)
    y_step(0, 1, 2)
    y_step(1, 0, 1)
    y_step(0, 0, 3)
    y_step(1, 1, 1)
    y_step(0, 1, 3)
    y_step(1, 0, 2)
    y_step(0, 0, 4)
    second_start(0, 0)
    y_step(1, 1, 2)
    y_step(0, 1, 4)
    second_start(0, 1)
    z_step(1, 0, 0, 1)
    y_step(1, 0, 3)
    z_step(1, 0, 1, 1)
    y_step(1, 1, 3)
    z_step(1, 0, 0, 2)
    z_step(1, 0, 1, 2)
    y_step(1, 0, 4)
    second_start(1, 0)
    z_step(1, 0, 0, 3)
    z_step(1, 0, 1, 3)
    y_step(1, 1, 4)
    second_start(1, 1)
    z_step(1, 0, 0, 4)
    z_step(1, 0, 1, 4)
    seconds(0)
    y_step(0, 2, 0)
    for s in range(1, 4):
        z_all(1, 1, s)
        y_step(0, 2, s)
    z_all(1, 1, 4)
    seconds(1)
    y_step(1, 2, 0)
    y_step(0, 2, 4)
    finish(0)
    for s in range(1, 5):
        y_step(1, 2, s)
    finish(1)
    for made in sent:
        made.wait_send()


def body(x_matrix, tangent, fill_x, fill_t):
    def partial_shapes(width):
        return [pltpu.VMEM((WIDTH, width), F32)] * 3

    def slot_shapes(width):
        return [pltpu.VMEM((2, 4, ROWS, width), F32)] * 3

    w0, w1 = HALVES[0][1], HALVES[1][1]
    vmem = pl.BlockSpec(memory_space=pltpu.VMEM)
    dma = pltpu.SemaphoreType.DMA
    return pl.pallas_call(
        kernel,
        out_shape=jax.ShapeDtypeStruct((ROWS, WIDTH), F32),
        in_specs=[vmem] * 4,
        out_specs=vmem,
        scratch_shapes=[
            pltpu.VMEM((2, N, PAD, 128), BF16),
            pltpu.VMEM((2, N, PAD, 128), BF16),
            pltpu.VMEM((2, N * PAD, LANES), BF16),
            pltpu.VMEM((2, LANES, N * PAD), BF16),
            pltpu.VMEM((2, N * PAD, w0), BF16),
            pltpu.VMEM((2, N * PAD, w1), BF16),
            pltpu.VMEM((2, N * PAD, w0), BF16),
            pltpu.VMEM((2, N * PAD, w1), BF16),
            *partial_shapes(w0), *partial_shapes(w1),
            *slot_shapes(w0), *slot_shapes(w1),
            pltpu.VMEM((ROWS, WIDTH), F32),
            dma((2, N)), dma((2, N)),
            dma((8, 2, 4)), dma((8, 2, 4)),
            dma((6, 2, 4)), dma((6, 2, 4)),
            dma((2, 2, 2)), dma((2, 2, 2)),
            dma((2, 4)), dma((2, 4)),
        ],
        compiler_params=pltpu.CompilerParams(
            collective_id=0, has_side_effects=True, vmem_limit_bytes=48 * 1024 * 1024
        ),
    )(x_matrix, tangent, fill_x, fill_t)


def solution(mesh):
    placed = (P(("row", "depth"), "col"), P(("row", "depth"), "col"), P(), P())
    return jax.shard_map(
        body, mesh=mesh, in_specs=placed, out_specs=P(("row", "depth"), "col"), check_vma=False
    )
```

time: 274 us -> 108 us (0.39)
  waiting for transfers between devices: 142 us -> 0 us
  Pallas kernels: 0 us -> 104 us
  local copies, waits for them, and re-layouts: 37.5 us -> 3.91 us
  other arithmetic: 30.4 us -> 0 us
  blocking collectives: 29.2 us -> 0 us
  between operations: 13.4 us -> 0.01 us
  starting transfers between devices: 11.1 us -> 0 us
  matrix products: 9.83 us -> 0 us
    pallas_call x0 -> x1, Pallas kernels: none -> 104 us  [body(): pl.pallas_call(kernel, out_shape=jax.ShapeDtypeStruct((ROWS, WIDTH), F32)...]
    unnamed x6 -> x0, waiting for transfers between devices: 90.8 us -> none
    all_gather x2 -> x0, waiting for transfers between devices: 49.2 us -> none  [right_panels(): received = lax.all_gather(stacked, 'row', axis=1, tiled=True)]
    all_to_all x1 -> x0, blocking collectives: 29.2 us -> none  [left_panels(): lax.all_to_all(tiled, ('col', 'depth'), split_axis=2, concat_axis=1, tile...]
    unnamed x1 -> x0, other arithmetic: 25.1 us -> none
    dot_general x7 -> x0, local copies, waits for them, and re-layouts: 11.7 us -> none  [partial_rows(): jnp.einsum('cdij,cjk->dik', left, right, preferred_element_type=jnp.float32)]
    all_to_all x1 -> x0, starting transfers between devices: 10.8 us -> none  [left_panels(): lax.all_to_all(tiled, ('col', 'depth'), split_axis=2, concat_axis=1, tile...]
    dot_general x9 -> x0, matrix products: 9.83 us -> none  [the longest x5 5.46 us: partial_rows(): jnp.einsum('cdij,cjk->dik', left, right, preferred_element_type=jnp.float32)]
  transfers between devices with their start and end apart: 5 -> 0, of which waited for: 4 -> 0; matrix products, arithmetic and copies ran while one was open for 15% -> 0% of each run, Pallas kernels for 0% -> 0%
where the time goes in v1:
time: 108 us
  Pallas kernels  104 us (96%)
  local copies, waits for them, and re-layouts  3.91 us (4%)
    pallas_call x1, Pallas kernels, body(): pl.pallas_call(kernel, out_shape=jax.ShapeDtypeStruct((ROWS, WIDTH), F32)...  104 us
    unnamed x9, local copies, waits for them, and re-layouts  3.91 us

profile of v1, /device:TPU:6, one launch (start us, length us, event | category | flops | bytes accessed | tf_op | source)
XLA Modules:
  0.0 108.2 jit_solution(16149184778512376953)
XLA Ops:
  0.0 0.0 copy-start
  0.0 0.9 copy-done
  0.9 0.0 copy-start.1
  0.9 0.9 copy-done.1
  1.8 0.0 copy-start.2
  1.8 0.7 copy-done.2
  2.5 0.0 copy-start.3
  2.5 0.7 copy-done.3
  3.2 104.3 %shard_map.46 = f32[72,576]{1,0:T(8,128)S(1)} custom-call(bf16[72,576]{1,0:T(8,128)(2,1)S(1)} %copy-done, bf16[72,576]{1,0:T(8,128)(2,1)S(1)} %copy-done.1, s32[36,36]{1,0:T(8,128)S(1)} %copy-done.2, s32[36,36]{1,0:T(8,128)S(1)} %copy-done.3), custom_call_target="tpu_custom_call" | custom-call | tf_op jit(solution)/shard_map/pallas_call | solution.py:315
  107.5 0.7 copy.6
Async XLA Ops:
  0.0 0.9 copy-start
  0.9 0.9 copy-start.1
  1.8 0.7 copy-start.2
  2.5 0.7 copy-start.3

commit v2 on v0

v2 whole, which is shorter than its diff:
```python
import jax
import jax.numpy as jnp
from jax import lax
from jax.experimental import pallas as pl
from jax.experimental.pallas import tpu as pltpu
from jax.sharding import PartitionSpec as P

MESH = pl.DeviceIdType.MESH
F32 = jnp.float32
BF16 = jnp.bfloat16
N = 8
NX = 4
ROWS = 72
PAD = 80
WIDTH = 576
LANES = 640
CHUNKS = ((0, 1, 0), (1, 1, 0), (2, 1, 0), (3, 1, 0), (4, 0, 1))
Z_TREES = ((3, 0), (3, 1), (4, 0), (4, 1))
Y_TREES = ((4, 2),)
RING_STEPS = ((4, 3), (3, 4))
ORDER = (
    ("prep", 0), ("z0", 0, 0, 0), ("a1", 0), ("prep", 1), ("z0", 1, 1, 0), ("z0", 0, 1, 0), ("a1", 1),
    ("z0", 1, 0, 0), ("z0", 0, 0, 1), ("z0", 1, 1, 1), ("a1f", 0), ("z0", 1, 0, 1), ("z0", 0, 1, 1),
    ("z0", 0, 0, 2), ("z0", 1, 1, 2), ("a1f", 1), ("z0", 1, 0, 2), ("x", 0, 3), ("z0", 0, 1, 2),
    ("z0", 0, 0, 3), ("x", 0, 1), ("z0", 1, 1, 3), ("x", 1, 2), ("x", 0, 2), ("z0", 1, 0, 3), ("x", 1, 3),
    ("left", 0), ("x", 1, 1), ("z0", 0, 1, 3), ("z0", 0, 0, 4), ("dot1", 2, 0), ("y", 2, 0, 1, 0),
    ("y", 2, 0, 0, 0), ("dot1", 1, 0), ("y", 1, 0, 1, 0), ("dot1", 0, 0), ("z0", 1, 1, 4),
    ("y", 0, 0, 0, 0), ("y", 1, 0, 0, 0), ("left", 1), ("y", 0, 0, 1, 0), ("dot1", 2, 1), ("y", 2, 1, 0, 0),
    ("y", 2, 1, 1, 0), ("dot1", 0, 1), ("dot1", 3, 0), ("y", 0, 1, 1, 0), ("y", 0, 1, 0, 0),
    ("y", 2, 0, 1, 1), ("y", 2, 0, 0, 1), ("dot1", 1, 1), ("y", 1, 0, 1, 1), ("y", 0, 0, 0, 1),
    ("y", 1, 1, 0, 0), ("y", 3, 0, 1, 0), ("y", 2, 1, 1, 1), ("y", 2, 1, 0, 1), ("dot1", 4, 1),
    ("dot1", 4, 0), ("y", 1, 0, 0, 1), ("y", 0, 1, 1, 1), ("y", 0, 0, 1, 1), ("y", 2, 0, 0, 2),
    ("y", 0, 0, 0, 2), ("y", 2, 0, 1, 2), ("y", 1, 1, 1, 0), ("y", 0, 1, 0, 1), ("y", 2, 1, 1, 2),
    ("y", 2, 1, 0, 2), ("y", 0, 1, 1, 2), ("y", 1, 1, 0, 1), ("y", 1, 0, 1, 2), ("y", 2, 0, 0, 3),
    ("y", 0, 0, 1, 2), ("dot1", 3, 1), ("y", 3, 0, 1, 1), ("y", 0, 0, 0, 3), ("y", 3, 0, 0, 0),
    ("y", 3, 1, 0, 0), ("y", 2, 0, 1, 3), ("y", 2, 1, 1, 3), ("y", 0, 1, 0, 2), ("y", 0, 1, 1, 3),
    ("y", 2, 0, 0, 4), ("sum", 2, 0), ("y", 1, 1, 1, 1), ("z1", 2, 0, 0, 0), ("y", 1, 0, 1, 3),
    ("y", 1, 1, 0, 2), ("y", 0, 0, 1, 3), ("y", 1, 0, 0, 2), ("y", 0, 0, 0, 4), ("y", 2, 1, 0, 3),
    ("sum", 0, 0), ("z1", 2, 0, 1, 0), ("z1", 0, 0, 0, 0), ("y", 3, 0, 1, 2), ("y", 3, 1, 1, 0),
    ("z1", 0, 0, 1, 0), ("y", 3, 0, 0, 1), ("y", 2, 1, 1, 4), ("sum", 2, 1), ("z1", 2, 1, 1, 0),
    ("z1", 2, 1, 0, 0), ("y", 3, 1, 0, 1), ("y", 0, 1, 1, 4), ("y", 0, 1, 0, 3), ("sum", 0, 1),
    ("z1", 0, 1, 1, 0), ("y", 4, 0, 0, 0), ("z1", 0, 1, 0, 0), ("z1", 2, 0, 0, 1), ("y", 1, 1, 1, 2),
    ("y", 4, 0, 1, 0), ("y", 1, 1, 0, 3), ("y", 4, 1, 0, 0), ("y", 4, 1, 1, 0), ("z1", 2, 0, 1, 1),
    ("y", 1, 0, 1, 4), ("y", 1, 0, 0, 3), ("sum", 1, 0), ("z1", 1, 0, 0, 0), ("z1", 0, 0, 0, 1),
    ("z1", 1, 0, 1, 0), ("y", 3, 0, 0, 2), ("z1", 0, 0, 1, 1), ("y", 3, 0, 1, 3), ("z1", 2, 1, 0, 1),
    ("y", 3, 1, 0, 2), ("y", 3, 1, 1, 1), ("z1", 2, 1, 1, 1), ("y", 4, 0, 0, 1), ("z1", 0, 1, 1, 1),
    ("z1", 0, 1, 0, 1), ("y", 1, 1, 1, 3), ("z1", 2, 0, 0, 2), ("y", 1, 1, 0, 4), ("sum", 1, 1),
    ("z1", 1, 1, 1, 0), ("z1", 1, 1, 0, 0), ("z1", 2, 0, 1, 2), ("y", 4, 1, 1, 1), ("y", 4, 0, 1, 1),
    ("z1", 1, 0, 0, 1), ("z1", 1, 0, 1, 1), ("z1", 0, 0, 0, 2), ("y", 3, 0, 0, 3), ("y", 3, 0, 1, 4),
    ("sum", 3, 0), ("y", 4, 1, 0, 1), ("zt", 3, 0, 0), ("y", 3, 1, 0, 3), ("y", 3, 1, 1, 2),
    ("z1", 0, 1, 0, 2), ("y", 4, 0, 0, 2), ("z1", 0, 1, 1, 2), ("z1", 1, 1, 1, 1), ("z1", 2, 1, 1, 2),
    ("y", 4, 1, 1, 2), ("z1", 1, 1, 0, 1), ("z1", 2, 0, 0, 3), ("z1", 1, 0, 0, 2), ("z1", 0, 0, 1, 2),
    ("y", 4, 1, 0, 2), ("z1", 2, 1, 0, 2), ("z1", 1, 0, 1, 2), ("y", 4, 0, 1, 2), ("y", 3, 1, 0, 4),
    ("y", 3, 1, 1, 3), ("sum", 3, 1), ("zt", 3, 1, 0), ("y", 4, 0, 0, 3), ("y", 4, 1, 1, 3),
    ("z1", 2, 0, 1, 3), ("z1", 0, 0, 0, 3), ("z1", 1, 1, 1, 2), ("z1", 2, 1, 1, 3), ("zt", 3, 0, 3),
    ("zt", 3, 0, 5), ("y", 4, 1, 0, 3), ("z1", 1, 1, 0, 2), ("z1", 0, 1, 1, 3), ("y", 4, 0, 1, 3),
    ("y", 4, 0, 0, 4), ("z1", 1, 0, 0, 3), ("z1", 1, 0, 1, 3), ("z1", 0, 1, 0, 3), ("sum", 4, 0),
    ("zt", 4, 0, 0), ("z1", 0, 0, 1, 3), ("y", 4, 1, 1, 4), ("z1", 2, 1, 0, 3), ("sum", 4, 1),
    ("z1", 2, 0, 0, 4), ("z1", 1, 1, 1, 3), ("zt", 3, 1, 3), ("z1", 2, 1, 1, 4), ("zt", 3, 1, 5),
    ("z1", 0, 0, 0, 4), ("zt", 4, 1, 0), ("dot2", 2), ("z1", 1, 1, 0, 3), ("z1", 0, 1, 1, 4), ("dot2", 0),
    ("z1", 1, 0, 0, 4), ("y", 2, 2, 1, 0), ("y", 0, 2, 1, 0), ("y", 0, 2, 0, 0), ("y", 2, 2, 0, 0),
    ("z1", 1, 1, 1, 4), ("dot2", 1), ("y", 1, 2, 0, 0), ("zt", 4, 0, 3), ("dot2", 3), ("y", 3, 2, 0, 0),
    ("y", 1, 2, 1, 0), ("y", 3, 2, 1, 0), ("y", 0, 2, 0, 1), ("zt", 4, 0, 5), ("y", 0, 2, 1, 1),
    ("zt", 4, 1, 5), ("y", 2, 2, 0, 1), ("zt", 4, 1, 3), ("y", 2, 2, 1, 1), ("y", 1, 2, 0, 1),
    ("y", 3, 2, 0, 1), ("y", 1, 2, 1, 1), ("y", 0, 2, 0, 2), ("y", 3, 2, 1, 1), ("y", 2, 2, 0, 2),
    ("y", 0, 2, 1, 2), ("dot2", 4), ("yt", 4, 2, 0), ("y", 3, 2, 0, 2), ("y", 1, 2, 1, 2),
    ("y", 3, 2, 1, 2), ("y", 2, 2, 1, 2), ("y", 1, 2, 0, 2), ("y", 0, 2, 1, 3), ("y", 0, 2, 0, 3),
    ("yt", 4, 2, 1), ("yt", 4, 2, 2), ("y", 2, 2, 0, 3), ("y", 1, 2, 1, 3), ("y", 3, 2, 1, 3),
    ("y", 1, 2, 0, 3), ("y", 2, 2, 1, 3), ("y", 3, 2, 0, 3), ("y", 0, 2, 0, 4), ("fin", 0),
    ("y", 2, 2, 0, 4), ("fin", 2), ("y", 1, 2, 1, 4), ("fin", 1), ("fin", 4), ("y", 3, 2, 1, 4), ("fin", 3),
)


def chunk_width(h):
    _, tiles, fold = CHUNKS[h]
    return tiles * 128 + fold * 64


def chunk_rows(h):
    _, tiles, fold = CHUNKS[h]
    return tiles * ROWS + fold * 40


def pack(value, h):
    _, tiles, fold = CHUNKS[h]
    rows = [value[:, t * 128 : (t + 1) * 128] for t in range(tiles)]
    if fold:
        last = value[:, tiles * 128 :]
        low = jnp.concatenate([last[40:], jnp.zeros((8, 64), F32)], axis=0)
        rows.append(jnp.concatenate([last[:40], low], axis=1))
    return rows[0] if len(rows) == 1 else jnp.concatenate(rows, axis=0)


def unpack(value, h):
    _, tiles, fold = CHUNKS[h]
    columns = [value[t * ROWS : (t + 1) * ROWS] for t in range(tiles)]
    if fold:
        last = value[tiles * ROWS :]
        columns.append(jnp.concatenate([last[:, :64], last[:32, 64:]], axis=0))
    return columns[0] if len(columns) == 1 else jnp.concatenate(columns, axis=1)


def kernel(x_hbm, t_hbm, fx_hbm, ft_hbm, out_ref, *scratch):
    scratch = list(scratch)
    ins = [scratch.pop(0) for _ in range(4)]
    a1_send, a1_recv, lt, left, tm, right0 = [scratch.pop(0) for _ in range(6)]
    rights = [scratch.pop(0) for _ in CHUNKS]
    parts = [scratch.pop(0) for _ in CHUNKS]
    slots = [scratch.pop(0) for _ in CHUNKS]
    in_s, a1_ss, a1_rs, x_ss, x_rs, c_rs, z0_ss, z0_rs, z_ss, z_rs, y_ss, y_rs = scratch

    r = lax.axis_index("row")
    c = lax.axis_index("col")
    d = lax.axis_index("depth")
    chip = c // 2
    core = lax.rem(c, 2)

    def wrap(value, size):
        return lax.rem(value + 2 * size, size)

    def at_row(step):
        return (wrap(r + step, N), c, d)

    def at_depth(step):
        return (r, c, wrap(d + step, N))

    def at_chip(step):
        return (r, wrap(chip + step, NX) * 2 + core, d)

    partner = (r, chip * 2 + 1 - core, d)

    barrier = pltpu.get_barrier_semaphore()
    greeted = [at_depth(s) for s in (4, 3, 5, 2, 6, 1, 7)]
    greeted += [at_row(s) for s in ((1, -1, 3, -3) if Z_TREES else (1, -1))]
    greeted += [at_chip(1), at_chip(2), at_chip(3), partner]
    for device in greeted:
        pl.semaphore_signal(barrier, inc=1, device_id=device, device_id_type=MESH)

    fetches = [
        pltpu.make_async_copy(src, dst, in_s.at[k])
        for k, (src, dst) in enumerate(zip((x_hbm, t_hbm, fx_hbm, ft_hbm), ins))
    ]
    for k in (0, 2, 1, 3):
        fetches[k].start()

    row_start = (r * N + d) * ROWS
    col_start = c * WIDTH

    def expand(fill):
        count = fill.shape[0]
        row_ids = (row_start + lax.broadcasted_iota(jnp.int32, (ROWS, count), 0)) >> 7
        row_hot = (row_ids == lax.broadcasted_iota(jnp.int32, (ROWS, count), 1)).astype(F32)
        col_ids = (col_start + lax.broadcasted_iota(jnp.int32, (count, WIDTH), 1)) >> 7
        col_hot = (col_ids == lax.broadcasted_iota(jnp.int32, (count, WIDTH), 0)).astype(F32)
        inner = jnp.dot(row_hot, fill.astype(F32), preferred_element_type=F32)
        return jnp.dot(inner, col_hot, preferred_element_type=F32)

    def chunk(index):
        return pl.ds(pl.multiple_of(index * PAD, 16), PAD)

    def tall(value):
        return jnp.concatenate([value, jnp.zeros((PAD - ROWS, value.shape[1]), F32)], axis=0)

    def copy(src, dst, send_sem, recv_sem, device):
        return pltpu.make_async_remote_copy(
            src_ref=src, dst_ref=dst, send_sem=send_sem, recv_sem=recv_sem,
            device_id=device, device_id_type=MESH,
        )

    def send(src, dst, send_sem, recv_sem, device):
        copy(src, dst, send_sem, recv_sem, device).start()

    def received(piece, recv_sem):
        copy(piece, piece, recv_sem, recv_sem, partner).wait_recv()

    def all_sent(pieces, send_sem):
        copy(pieces, pieces, send_sem, send_sem, partner).wait_send()

    def prep(m):
        fetches[m].wait()
        fetches[2 + m].wait()
        masked = ins[m][...].astype(F32) * expand(ins[2 + m][...])
        if m == 1:
            tm[...] = masked
        padded = tall(masked)
        for j in range(N):
            piece = padded[:, j * ROWS : (j + 1) * ROWS]
            wide = jnp.concatenate([piece, jnp.zeros((PAD, 128 - ROWS), F32)], axis=1)
            a1_send[m, j] = wide.astype(BF16)
        right0[m, chunk(r), :] = padded.astype(BF16)
        a1_recv[m, d] = a1_send[m, d]
        if m == 0:
            pl.semaphore_wait(barrier, len(greeted))

    def a1(m):
        for s in (4, 3, 5, 2, 6, 1, 7):
            to = wrap(d + s, N)
            send(a1_send.at[m, to], a1_recv.at[m, d], a1_ss.at[m], a1_rs.at[m], (r, c, to))

    def lt_piece(m, owner_chip, owner_core):
        return lt.at[m, chunk(wrap(owner_chip, NX) * 2 + owner_core), :]

    def a1f(m):
        received(a1_recv.at[m, pl.ds(0, N - 1)], a1_rs.at[m])
        stacked = a1_recv[m].astype(F32)[:, :ROWS, :].reshape(N * ROWS, 128)
        turned = tall(jnp.transpose(stacked)[:ROWS])
        turned = jnp.concatenate([turned, jnp.zeros((PAD, LANES - WIDTH), F32)], axis=1)
        lt[m, chunk(c), :] = turned.astype(BF16)
        piece = lt_piece(m, chip, core)
        for q in (2, 1, 3):
            send(piece, piece, x_ss.at[m], x_rs.at[m, q - 1], at_chip(q))
        send(piece, piece, x_ss.at[m], c_rs.at[m], partner)

    def x(m, q):
        piece = lt_piece(m, chip - q, core)
        received(piece, x_rs.at[m, q - 1])
        send(piece, piece, x_ss.at[m], c_rs.at[m], partner)

    def left_panel(m):
        received(lt.at[m, pl.ds(0, NX * PAD), :], c_rs.at[m])
        for i in range(LANES // 128):
            lanes = slice(i * 128, (i + 1) * 128)
            left[m, lanes, :] = jnp.transpose(lt[m, :, lanes].astype(F32)).astype(BF16)

    def ring(buf, send_sem, recv_sems, m, e, s):
        sign, steps = (1, -1)[e], RING_STEPS[m][e]
        at = e * RING_STEPS[m][0]
        piece = buf.at[m, chunk(wrap(r - sign * s, N)), :]
        if s > 0:
            received(piece, recv_sems.at[at + s - 1])
        if s < steps:
            send(piece, piece, send_sem, recv_sems.at[at + s], at_row(sign))

    def z0(m, e, s):
        ring(right0, z0_ss.at[m], z0_rs.at[m], m, e, s)

    def z1(h, m, e, s):
        ring(rights[h], z_ss.at[h, m], z_rs.at[h, m], m, e, s)

    def zt(h, m, q):
        piece = rights[h].at[m, chunk(wrap(r - q, N)), :]
        if q > 0:
            received(piece, z_rs.at[h, m, q - 1])
        for step in {0: (3, -3, 1, -1), 3: (1, -1), 5: (1,)}[q]:
            there = (q + step) % N
            send(piece, piece, z_ss.at[h, m], z_rs.at[h, m, there - 1], at_row(step))

    def y(h, k, e, s):
        sign, (plus, minus) = (1, -1)[e], RING_STEPS[(k + h) % 2]
        steps = (plus, minus)[e]
        part, slot, at = parts[h], slots[h], 7 * k + e * plus
        dest = wrap(d + sign * (steps - s), N)
        if s > 0:
            received(slot.at[at + s - 1], y_rs.at[h, at + s - 1])
            if s < steps:
                slot[at + s - 1] = slot[at + s - 1] + part[k, dest]
        if s < steps:
            source = part.at[k, dest] if s == 0 else slot.at[at + s - 1]
            send(source, slot.at[at + s], y_ss.at[h], y_rs.at[h, at + s], at_depth(sign))

    def yt(h, k, stage):
        part, slot, at = parts[h], slots[h], 7 * k

        def go(source, index, step):
            send(source, slot.at[at + index], y_ss.at[h], y_rs.at[h, at + index], at_depth(step))

        def mine(step):
            return wrap(d + step, N)

        if stage == 0:
            for index, (away, step) in enumerate(((4, 1), (2, -1), (-2, 1), (1, 1), (-1, -1))):
                go(part.at[k, mine(away)], index, step)
        elif stage == 1:
            for index in (0, 1):
                received(slot.at[at + index], y_rs.at[h, at + index])
            slot[at] = slot[at] + slot[at + 1] + part[k, mine(3)]
            go(slot.at[at], 5, 3)
        else:
            received(slot.at[at + 2], y_rs.at[h, at + 2])
            slot[at + 2] = slot[at + 2] + part[k, mine(-3)]
            go(slot.at[at + 2], 6, -3)

    def y_total(h, k):
        at = 7 * k
        if (h, k) in Y_TREES:
            last = (3, 4, 5, 6)
            for index in last:
                received(slots[h].at[at + index], y_rs.at[h, at + index])
        else:
            last = (RING_STEPS[(k + h) % 2][0] - 1, 6)
        total = parts[h][k, d]
        for index in last:
            total = total + slots[h][at + index]
        return unpack(total, h)

    def multiply(h, k, terms):
        blocks = 4
        tile = blocks * ROWS

        def one(i, carry):
            rows = pl.ds(pl.multiple_of(i * tile, 16), tile)
            total = None
            for m, right in terms:
                term = jnp.dot(left[m, rows, :], right[...], preferred_element_type=F32)
                total = term if total is None else total + term
            for b in range(blocks):
                parts[h][k, i * blocks + b] = pack(total[b * ROWS : (b + 1) * ROWS], h)
            return carry

        lax.fori_loop(0, N // blocks, one, 0)

    def lanes_of(h):
        start = CHUNKS[h][0] * 128
        return slice(start, start + chunk_width(h))

    def dot1(h, k):
        right_x, right_t = (right0.at[m, :, lanes_of(h)] for m in range(2))
        multiply(h, k, ((0, right_x),) if k == 0 else ((1, right_x), (0, right_t)))

    def sum1(h, k):
        rights[h][k, chunk(r), :] = tall(y_total(h, k)).astype(BF16)

    def dot2(h):
        for m in range(2):
            if (h, m) in Z_TREES:
                for q in (1, 2, 4, 6, 7):
                    piece = rights[h].at[m, chunk(wrap(r - q, N)), :]
                    received(piece, z_rs.at[h, m, q - 1])
        multiply(h, 2, ((1, rights[h].at[0]), (0, rights[h].at[1])))

    def fin(h):
        lanes = lanes_of(h)
        out_ref[:, lanes] = 1.5 * tm[:, lanes] - 0.5 * y_total(h, 2)

    steps = {
        "prep": prep, "a1": a1, "a1f": a1f, "x": x, "left": left_panel, "z0": z0, "z1": z1, "zt": zt,
        "y": y, "yt": yt, "dot1": dot1, "sum": sum1, "dot2": dot2, "fin": fin,
    }
    for name, *which in ORDER:
        steps[name](*which)

    for m in range(2):
        all_sent(a1_send.at[m, pl.ds(0, N - 1)], a1_ss.at[m])
        all_sent(lt.at[m, pl.ds(0, 7 * PAD), :], x_ss.at[m])
        all_sent(right0.at[m, pl.ds(0, 7 * PAD), :], z0_ss.at[m])
        for h in range(len(CHUNKS)):
            all_sent(rights[h].at[m, pl.ds(0, 7 * PAD), :], z_ss.at[h, m])
    for h in range(len(CHUNKS)):
        all_sent(slots[h], y_ss.at[h])


def body(x_matrix, tangent, fill_x, fill_t):
    count = len(CHUNKS)
    vmem = pltpu.VMEM
    dma = pltpu.SemaphoreType.DMA
    hbm = pl.BlockSpec(memory_space=pl.ANY)
    return pl.pallas_call(
        kernel,
        out_shape=jax.ShapeDtypeStruct((ROWS, WIDTH), F32),
        in_specs=[hbm] * 4,
        out_specs=pl.BlockSpec(memory_space=vmem),
        scratch_shapes=[
            *[vmem(a.shape, a.dtype) for a in (x_matrix, tangent, fill_x, fill_t)],
            vmem((2, N, PAD, 128), BF16),
            vmem((2, N, PAD, 128), BF16),
            vmem((2, N * PAD, LANES), BF16),
            vmem((2, LANES, N * PAD), BF16),
            vmem((ROWS, WIDTH), F32),
            vmem((2, N * PAD, WIDTH), BF16),
            *[vmem((2, N * PAD, chunk_width(h)), BF16) for h in range(count)],
            *[vmem((3, N, chunk_rows(h), 128), F32) for h in range(count)],
            *[vmem((3 * 7, chunk_rows(h), 128), F32) for h in range(count)],
            dma((4,)),
            dma((2,)), dma((2,)),
            dma((2,)), dma((2, 3)), dma((2,)),
            dma((2,)), dma((2, 7)),
            dma((count, 2)), dma((count, 2, 7)),
            dma((count,)), dma((count, 3 * 7)),
        ],
        compiler_params=pltpu.CompilerParams(
            collective_id=0, has_side_effects=True, vmem_limit_bytes=60 * 1024 * 1024
        ),
    )(x_matrix, tangent, fill_x, fill_t)


def solution(mesh):
    placed = (P(("row", "depth"), "col"), P(("row", "depth"), "col"), P(), P())
    return jax.shard_map(
        body, mesh=mesh, in_specs=placed, out_specs=P(("row", "depth"), "col"), check_vma=False
    )
```

time: 274 us -> 90.7 us (0.33)
  waiting for transfers between devices: 142 us -> 0 us
  Pallas kernels: 0 us -> 88 us
  local copies, waits for them, and re-layouts: 37.5 us -> 1.61 us
  other arithmetic: 30.4 us -> 0 us
  blocking collectives: 29.2 us -> 0 us
  between operations: 13.4 us -> 0.01 us
  starting transfers between devices: 11.1 us -> 0 us
  matrix products: 9.83 us -> 0 us
    unnamed x6 -> x0, waiting for transfers between devices: 90.8 us -> none
    pallas_call x0 -> x1, Pallas kernels: none -> 88 us  [body(): pl.pallas_call(kernel, out_shape=jax.ShapeDtypeStruct((ROWS, WIDTH), F32)...]
    all_gather x2 -> x0, waiting for transfers between devices: 49.2 us -> none  [right_panels(): received = lax.all_gather(stacked, 'row', axis=1, tiled=True)]
    all_to_all x1 -> x0, blocking collectives: 29.2 us -> none  [left_panels(): lax.all_to_all(tiled, ('col', 'depth'), split_axis=2, concat_axis=1, tile...]
    unnamed x1 -> x0, other arithmetic: 25.1 us -> none
    dot_general x7 -> x0, local copies, waits for them, and re-layouts: 11.7 us -> none  [partial_rows(): jnp.einsum('cdij,cjk->dik', left, right, preferred_element_type=jnp.float32)]
    all_to_all x1 -> x0, starting transfers between devices: 10.8 us -> none  [left_panels(): lax.all_to_all(tiled, ('col', 'depth'), split_axis=2, concat_axis=1, tile...]
    dot_general x9 -> x0, matrix products: 9.83 us -> none  [the longest x5 5.46 us: partial_rows(): jnp.einsum('cdij,cjk->dik', left, right, preferred_element_type=jnp.float32)]
  transfers between devices with their start and end apart: 5 -> 0, of which waited for: 4 -> 0; matrix products, arithmetic and copies ran while one was open for 15% -> 0% of each run, Pallas kernels for 0% -> 0%
where the time goes in v2:
time: 90.7 us; the launch traced here: 89.6 us
  Pallas kernels  88 us (97%)
  local copies, waits for them, and re-layouts  1.61 us (2%)
    pallas_call x1, Pallas kernels, body(): pl.pallas_call(kernel, out_shape=jax.ShapeDtypeStruct((ROWS, WIDTH), F32)...  88 us

profile of v2, /device:TPU:6, one launch (start us, length us, event | category | flops | bytes accessed | tf_op | source)
XLA Modules:
  0.0 89.6 jit_solution(3839463179846757567)
XLA Ops:
  0.0 88.0 %shard_map.46 = f32[72,576]{1,0:T(8,128)} custom-call(bf16[72,576]{1,0:T(8,128)(2,1)} %x_hbm.1, bf16[72,576]{1,0:T(8,128)(2,1)} %t_hbm.1, s32[36,36]{1,0:T(8,128)} %fx_hbm.1, s32[36,36]{1,0:T(8,128)} %ft_hbm.1), custom_call_target="tpu_custom_call" | custom-call | tf_op jit(solution)/shard_map/pallas_call | solution.py:357
  88.0 1.6 %copy.6 = f32[72,576]{1,0:T(8,128)} copy(f32[72,576]{1,0:T(8,128)} %shard_map.46) | data formatting | bytes 331776

commit v3 on v2

--- a/solution.py
+++ b/solution.py
@@ -18,56 +18,59 @@
 Z_TREES = ((3, 0), (3, 1), (4, 0), (4, 1))
 Y_TREES = ((4, 2),)
 RING_STEPS = ((4, 3), (3, 4))
+SHORT = 2
 ORDER = (
-    ("prep", 0), ("z0", 0, 0, 0), ("a1", 0), ("prep", 1), ("z0", 1, 1, 0), ("z0", 0, 1, 0), ("a1", 1),
-    ("z0", 1, 0, 0), ("z0", 0, 0, 1), ("z0", 1, 1, 1), ("a1f", 0), ("z0", 1, 0, 1), ("z0", 0, 1, 1),
-    ("z0", 0, 0, 2), ("z0", 1, 1, 2), ("a1f", 1), ("z0", 1, 0, 2), ("x", 0, 3), ("z0", 0, 1, 2),
-    ("z0", 0, 0, 3), ("x", 0, 1), ("z0", 1, 1, 3), ("x", 1, 2), ("x", 0, 2), ("z0", 1, 0, 3), ("x", 1, 3),
-    ("left", 0), ("x", 1, 1), ("z0", 0, 1, 3), ("z0", 0, 0, 4), ("dot1", 2, 0), ("y", 2, 0, 1, 0),
-    ("y", 2, 0, 0, 0), ("dot1", 1, 0), ("y", 1, 0, 1, 0), ("dot1", 0, 0), ("z0", 1, 1, 4),
-    ("y", 0, 0, 0, 0), ("y", 1, 0, 0, 0), ("left", 1), ("y", 0, 0, 1, 0), ("dot1", 2, 1), ("y", 2, 1, 0, 0),
-    ("y", 2, 1, 1, 0), ("dot1", 0, 1), ("dot1", 3, 0), ("y", 0, 1, 1, 0), ("y", 0, 1, 0, 0),
-    ("y", 2, 0, 1, 1), ("y", 2, 0, 0, 1), ("dot1", 1, 1), ("y", 1, 0, 1, 1), ("y", 0, 0, 0, 1),
-    ("y", 1, 1, 0, 0), ("y", 3, 0, 1, 0), ("y", 2, 1, 1, 1), ("y", 2, 1, 0, 1), ("dot1", 4, 1),
-    ("dot1", 4, 0), ("y", 1, 0, 0, 1), ("y", 0, 1, 1, 1), ("y", 0, 0, 1, 1), ("y", 2, 0, 0, 2),
-    ("y", 0, 0, 0, 2), ("y", 2, 0, 1, 2), ("y", 1, 1, 1, 0), ("y", 0, 1, 0, 1), ("y", 2, 1, 1, 2),
-    ("y", 2, 1, 0, 2), ("y", 0, 1, 1, 2), ("y", 1, 1, 0, 1), ("y", 1, 0, 1, 2), ("y", 2, 0, 0, 3),
-    ("y", 0, 0, 1, 2), ("dot1", 3, 1), ("y", 3, 0, 1, 1), ("y", 0, 0, 0, 3), ("y", 3, 0, 0, 0),
-    ("y", 3, 1, 0, 0), ("y", 2, 0, 1, 3), ("y", 2, 1, 1, 3), ("y", 0, 1, 0, 2), ("y", 0, 1, 1, 3),
-    ("y", 2, 0, 0, 4), ("sum", 2, 0), ("y", 1, 1, 1, 1), ("z1", 2, 0, 0, 0), ("y", 1, 0, 1, 3),
-    ("y", 1, 1, 0, 2), ("y", 0, 0, 1, 3), ("y", 1, 0, 0, 2), ("y", 0, 0, 0, 4), ("y", 2, 1, 0, 3),
-    ("sum", 0, 0), ("z1", 2, 0, 1, 0), ("z1", 0, 0, 0, 0), ("y", 3, 0, 1, 2), ("y", 3, 1, 1, 0),
-    ("z1", 0, 0, 1, 0), ("y", 3, 0, 0, 1), ("y", 2, 1, 1, 4), ("sum", 2, 1), ("z1", 2, 1, 1, 0),
-    ("z1", 2, 1, 0, 0), ("y", 3, 1, 0, 1), ("y", 0, 1, 1, 4), ("y", 0, 1, 0, 3), ("sum", 0, 1),
-    ("z1", 0, 1, 1, 0), ("y", 4, 0, 0, 0), ("z1", 0, 1, 0, 0), ("z1", 2, 0, 0, 1), ("y", 1, 1, 1, 2),
-    ("y", 4, 0, 1, 0), ("y", 1, 1, 0, 3), ("y", 4, 1, 0, 0), ("y", 4, 1, 1, 0), ("z1", 2, 0, 1, 1),
-    ("y", 1, 0, 1, 4), ("y", 1, 0, 0, 3), ("sum", 1, 0), ("z1", 1, 0, 0, 0), ("z1", 0, 0, 0, 1),
-    ("z1", 1, 0, 1, 0), ("y", 3, 0, 0, 2), ("z1", 0, 0, 1, 1), ("y", 3, 0, 1, 3), ("z1", 2, 1, 0, 1),
-    ("y", 3, 1, 0, 2), ("y", 3, 1, 1, 1), ("z1", 2, 1, 1, 1), ("y", 4, 0, 0, 1), ("z1", 0, 1, 1, 1),
-    ("z1", 0, 1, 0, 1), ("y", 1, 1, 1, 3), ("z1", 2, 0, 0, 2), ("y", 1, 1, 0, 4), ("sum", 1, 1),
-    ("z1", 1, 1, 1, 0), ("z1", 1, 1, 0, 0), ("z1", 2, 0, 1, 2), ("y", 4, 1, 1, 1), ("y", 4, 0, 1, 1),
-    ("z1", 1, 0, 0, 1), ("z1", 1, 0, 1, 1), ("z1", 0, 0, 0, 2), ("y", 3, 0, 0, 3), ("y", 3, 0, 1, 4),
-    ("sum", 3, 0), ("y", 4, 1, 0, 1), ("zt", 3, 0, 0), ("y", 3, 1, 0, 3), ("y", 3, 1, 1, 2),
-    ("z1", 0, 1, 0, 2), ("y", 4, 0, 0, 2), ("z1", 0, 1, 1, 2), ("z1", 1, 1, 1, 1), ("z1", 2, 1, 1, 2),
-    ("y", 4, 1, 1, 2), ("z1", 1, 1, 0, 1), ("z1", 2, 0, 0, 3), ("z1", 1, 0, 0, 2), ("z1", 0, 0, 1, 2),
-    ("y", 4, 1, 0, 2), ("z1", 2, 1, 0, 2), ("z1", 1, 0, 1, 2), ("y", 4, 0, 1, 2), ("y", 3, 1, 0, 4),
-    ("y", 3, 1, 1, 3), ("sum", 3, 1), ("zt", 3, 1, 0), ("y", 4, 0, 0, 3), ("y", 4, 1, 1, 3),
-    ("z1", 2, 0, 1, 3), ("z1", 0, 0, 0, 3), ("z1", 1, 1, 1, 2), ("z1", 2, 1, 1, 3), ("zt", 3, 0, 3),
-    ("zt", 3, 0, 5), ("y", 4, 1, 0, 3), ("z1", 1, 1, 0, 2), ("z1", 0, 1, 1, 3), ("y", 4, 0, 1, 3),
-    ("y", 4, 0, 0, 4), ("z1", 1, 0, 0, 3), ("z1", 1, 0, 1, 3), ("z1", 0, 1, 0, 3), ("sum", 4, 0),
-    ("zt", 4, 0, 0), ("z1", 0, 0, 1, 3), ("y", 4, 1, 1, 4), ("z1", 2, 1, 0, 3), ("sum", 4, 1),
-    ("z1", 2, 0, 0, 4), ("z1", 1, 1, 1, 3), ("zt", 3, 1, 3), ("z1", 2, 1, 1, 4), ("zt", 3, 1, 5),
-    ("z1", 0, 0, 0, 4), ("zt", 4, 1, 0), ("dot2", 2), ("z1", 1, 1, 0, 3), ("z1", 0, 1, 1, 4), ("dot2", 0),
-    ("z1", 1, 0, 0, 4), ("y", 2, 2, 1, 0), ("y", 0, 2, 1, 0), ("y", 0, 2, 0, 0), ("y", 2, 2, 0, 0),
-    ("z1", 1, 1, 1, 4), ("dot2", 1), ("y", 1, 2, 0, 0), ("zt", 4, 0, 3), ("dot2", 3), ("y", 3, 2, 0, 0),
-    ("y", 1, 2, 1, 0), ("y", 3, 2, 1, 0), ("y", 0, 2, 0, 1), ("zt", 4, 0, 5), ("y", 0, 2, 1, 1),
-    ("zt", 4, 1, 5), ("y", 2, 2, 0, 1), ("zt", 4, 1, 3), ("y", 2, 2, 1, 1), ("y", 1, 2, 0, 1),
-    ("y", 3, 2, 0, 1), ("y", 1, 2, 1, 1), ("y", 0, 2, 0, 2), ("y", 3, 2, 1, 1), ("y", 2, 2, 0, 2),
-    ("y", 0, 2, 1, 2), ("dot2", 4), ("yt", 4, 2, 0), ("y", 3, 2, 0, 2), ("y", 1, 2, 1, 2),
-    ("y", 3, 2, 1, 2), ("y", 2, 2, 1, 2), ("y", 1, 2, 0, 2), ("y", 0, 2, 1, 3), ("y", 0, 2, 0, 3),
-    ("yt", 4, 2, 1), ("yt", 4, 2, 2), ("y", 2, 2, 0, 3), ("y", 1, 2, 1, 3), ("y", 3, 2, 1, 3),
-    ("y", 1, 2, 0, 3), ("y", 2, 2, 1, 3), ("y", 3, 2, 0, 3), ("y", 0, 2, 0, 4), ("fin", 0),
-    ("y", 2, 2, 0, 4), ("fin", 2), ("y", 1, 2, 1, 4), ("fin", 1), ("fin", 4), ("y", 3, 2, 1, 4), ("fin", 3),
+    ("prep", 0), ("a1", 0), ("prep", 1), ("z0", 1, 1, 0), ("z0", 2, 0, 0), ("z0", 0, 0, 0), ("a1", 1),
+    ("z0", 0, 1, 0), ("z0", 1, 0, 0), ("z0", 2, 0, 1), ("z0", 1, 1, 1), ("z0", 2, 1, 0), ("z0", 0, 0, 1),
+    ("z0", 2, 0, 2), ("a1f", 0), ("z0", 1, 0, 1), ("z0", 0, 1, 1), ("z0", 1, 1, 2), ("z0", 2, 1, 1),
+    ("z0", 0, 0, 2), ("a1f", 1), ("z0", 0, 1, 2), ("z0", 1, 0, 2), ("z0", 1, 1, 3), ("z0", 2, 0, 3),
+    ("x", 0, 3), ("x", 0, 2), ("z0", 0, 0, 3), ("x", 0, 1), ("z0", 1, 0, 3), ("left", 0), ("x", 1, 2),
+    ("z0", 2, 0, 4), ("x", 1, 1), ("z0", 1, 1, 4), ("dot1", 3, 0), ("y", 3, 0, 1, 0), ("y", 3, 0, 0, 0),
+    ("dot1", 2, 0), ("x", 1, 3), ("z0", 0, 1, 3), ("y", 2, 0, 1, 0), ("y", 2, 0, 0, 0), ("z0", 0, 0, 4),
+    ("dot1", 0, 0), ("dot1", 1, 0), ("y", 0, 0, 0, 0), ("y", 1, 0, 0, 0), ("y", 0, 0, 1, 0),
+    ("y", 1, 0, 1, 0), ("left", 1), ("dot1", 0, 1), ("y", 0, 1, 0, 0), ("z0", 2, 1, 2), ("y", 0, 1, 1, 0),
+    ("y", 3, 0, 0, 1), ("y", 3, 0, 1, 1), ("dot1", 3, 1), ("y", 2, 0, 0, 1), ("y", 3, 1, 0, 0),
+    ("y", 2, 0, 1, 1), ("dot1", 1, 1), ("y", 0, 0, 1, 1), ("y", 1, 1, 1, 0), ("y", 0, 0, 0, 1),
+    ("dot1", 2, 1), ("y", 1, 1, 0, 0), ("y", 0, 1, 1, 1), ("y", 2, 1, 0, 0), ("y", 0, 1, 0, 1),
+    ("y", 2, 1, 1, 0), ("y", 3, 0, 1, 2), ("y", 1, 0, 0, 1), ("y", 1, 0, 1, 1), ("z0", 2, 1, 3),
+    ("y", 2, 0, 1, 2), ("dot1", 4, 1), ("y", 2, 0, 0, 2), ("y", 0, 0, 0, 2), ("y", 0, 1, 1, 2),
+    ("y", 2, 1, 1, 1), ("y", 0, 0, 1, 2), ("y", 3, 1, 1, 0), ("y", 1, 1, 0, 1), ("y", 0, 1, 0, 2),
+    ("dot1", 4, 0), ("y", 3, 1, 0, 1), ("y", 1, 0, 1, 2), ("y", 3, 0, 0, 2), ("y", 2, 0, 0, 3),
+    ("y", 1, 1, 1, 1), ("y", 0, 1, 1, 3), ("y", 0, 0, 0, 3), ("y", 2, 1, 1, 2), ("y", 2, 0, 1, 3),
+    ("y", 2, 1, 0, 1), ("y", 1, 1, 0, 2), ("y", 3, 0, 1, 3), ("y", 4, 1, 1, 0), ("y", 4, 1, 0, 0),
+    ("y", 3, 1, 0, 2), ("y", 4, 0, 0, 0), ("y", 3, 1, 1, 1), ("y", 1, 0, 0, 2), ("y", 1, 1, 1, 2),
+    ("y", 2, 0, 0, 4), ("sum", 2, 0), ("z1", 2, 0, 0, 0), ("y", 0, 0, 1, 3), ("z1", 2, 0, 1, 0),
+    ("y", 0, 1, 0, 3), ("y", 0, 1, 1, 4), ("sum", 0, 1), ("z1", 0, 1, 1, 0), ("y", 0, 0, 0, 4),
+    ("z1", 0, 1, 0, 0), ("sum", 0, 0), ("y", 1, 0, 1, 3), ("z1", 0, 0, 1, 0), ("z1", 0, 0, 0, 0),
+    ("y", 3, 0, 0, 3), ("y", 2, 1, 1, 3), ("y", 2, 1, 0, 2), ("y", 3, 0, 1, 4), ("sum", 3, 0),
+    ("zt", 3, 0, 0), ("y", 1, 1, 0, 3), ("y", 4, 1, 1, 1), ("y", 3, 1, 1, 2), ("y", 3, 1, 0, 3),
+    ("z1", 2, 0, 1, 1), ("z1", 2, 0, 0, 1), ("y", 4, 0, 1, 0), ("y", 1, 1, 1, 3), ("y", 4, 0, 0, 1),
+    ("z1", 0, 1, 1, 1), ("y", 1, 0, 1, 4), ("z1", 0, 1, 0, 1), ("y", 1, 0, 0, 3), ("sum", 1, 0),
+    ("z1", 0, 0, 0, 1), ("z1", 0, 0, 1, 1), ("y", 2, 1, 1, 4), ("y", 2, 1, 0, 3), ("z1", 1, 0, 0, 0),
+    ("sum", 2, 1), ("z1", 2, 1, 1, 0), ("y", 1, 1, 0, 4), ("sum", 1, 1), ("z1", 2, 1, 0, 0),
+    ("z1", 1, 1, 1, 0), ("y", 4, 1, 0, 1), ("z1", 1, 0, 1, 0), ("y", 4, 1, 1, 2), ("y", 3, 1, 1, 3),
+    ("z1", 1, 1, 0, 0), ("y", 3, 1, 0, 4), ("sum", 3, 1), ("zt", 3, 1, 0), ("y", 4, 0, 1, 1),
+    ("z1", 2, 0, 0, 2), ("y", 4, 0, 0, 2), ("z1", 0, 1, 1, 2), ("z1", 1, 0, 0, 1), ("z1", 2, 1, 1, 1),
+    ("z1", 0, 0, 0, 2), ("z1", 2, 1, 0, 1), ("z1", 1, 1, 1, 1), ("y", 4, 0, 1, 2), ("z1", 0, 0, 1, 2),
+    ("z1", 0, 1, 0, 2), ("z1", 1, 1, 0, 1), ("z1", 1, 0, 1, 1), ("zt", 3, 0, 3), ("y", 4, 1, 1, 3),
+    ("y", 4, 1, 0, 2), ("y", 4, 0, 0, 3), ("zt", 3, 0, 5), ("z1", 2, 0, 1, 2), ("z1", 2, 0, 0, 3),
+    ("z1", 0, 1, 1, 3), ("zt", 3, 1, 5), ("z1", 2, 1, 1, 2), ("z1", 1, 0, 0, 2), ("z1", 1, 1, 1, 2),
+    ("zt", 3, 1, 3), ("z1", 0, 0, 0, 3), ("y", 4, 1, 0, 3), ("y", 4, 1, 1, 4), ("z1", 2, 1, 0, 2),
+    ("z1", 1, 0, 1, 2), ("sum", 4, 1), ("z1", 0, 1, 0, 3), ("zt", 4, 1, 0), ("y", 4, 0, 0, 4),
+    ("z1", 0, 0, 1, 3), ("z1", 2, 1, 1, 3), ("y", 4, 0, 1, 3), ("z1", 2, 0, 0, 4), ("z1", 1, 1, 0, 2),
+    ("z1", 1, 1, 1, 3), ("sum", 4, 0), ("z1", 1, 0, 0, 3), ("z1", 0, 1, 1, 4), ("zt", 4, 0, 0), ("dot2", 3),
+    ("y", 3, 2, 0, 0), ("z1", 2, 1, 0, 3), ("z1", 0, 0, 0, 4), ("dot2", 0), ("z1", 1, 0, 1, 3),
+    ("y", 0, 2, 1, 0), ("y", 3, 2, 1, 0), ("y", 0, 2, 0, 0), ("z1", 2, 0, 1, 3), ("z1", 2, 1, 1, 4),
+    ("dot2", 2), ("z1", 1, 1, 1, 4), ("y", 2, 2, 0, 0), ("y", 2, 2, 1, 0), ("zt", 4, 1, 3),
+    ("z1", 1, 1, 0, 3), ("zt", 4, 1, 5), ("z1", 1, 0, 0, 4), ("dot2", 1), ("y", 1, 2, 1, 0),
+    ("y", 3, 2, 0, 1), ("y", 0, 2, 1, 1), ("y", 1, 2, 0, 0), ("y", 0, 2, 0, 1), ("zt", 4, 0, 5),
+    ("y", 3, 2, 1, 1), ("zt", 4, 0, 3), ("y", 2, 2, 0, 1), ("y", 2, 2, 1, 1), ("y", 3, 2, 0, 2),
+    ("y", 1, 2, 1, 1), ("y", 0, 2, 1, 2), ("y", 1, 2, 0, 1), ("y", 3, 2, 1, 2), ("y", 0, 2, 0, 2),
+    ("dot2", 4), ("yt", 4, 2, 0), ("y", 2, 2, 0, 2), ("y", 1, 2, 1, 2), ("y", 3, 2, 0, 3),
+    ("y", 2, 2, 1, 2), ("y", 1, 2, 0, 2), ("y", 3, 2, 1, 3), ("yt", 4, 2, 1), ("y", 0, 2, 0, 3),
+    ("yt", 4, 2, 2), ("y", 1, 2, 1, 3), ("y", 2, 2, 0, 3), ("y", 2, 2, 1, 3), ("y", 3, 2, 1, 4),
+    ("y", 0, 2, 1, 3), ("y", 0, 2, 0, 4), ("fin", 0), ("fin", 3), ("y", 1, 2, 1, 4), ("y", 1, 2, 0, 3),
+    ("fin", 1), ("y", 2, 2, 0, 4), ("fin", 2), ("fin", 4),
 )
 
 
@@ -103,11 +106,12 @@
 def kernel(x_hbm, t_hbm, fx_hbm, ft_hbm, out_ref, *scratch):
     scratch = list(scratch)
     ins = [scratch.pop(0) for _ in range(4)]
-    a1_send, a1_recv, lt, left, tm, right0 = [scratch.pop(0) for _ in range(6)]
+    a1_send, a1_recv, lt, left, xm, tm, pairs, ends = [scratch.pop(0) for _ in range(8)]
     rights = [scratch.pop(0) for _ in CHUNKS]
     parts = [scratch.pop(0) for _ in CHUNKS]
     slots = [scratch.pop(0) for _ in CHUNKS]
-    in_s, a1_ss, a1_rs, x_ss, x_rs, c_rs, z0_ss, z0_rs, z_ss, z_rs, y_ss, y_rs = scratch
+    shorts = [scratch.pop(0) for _ in CHUNKS]
+    in_s, a1_ss, a1_rs, x_ss, x_rs, c_rs, z0_ss, z0_rs, z_ss, z_rs, y_ss, y_rs, b_ss = scratch
 
     r = lax.axis_index("row")
     c = lax.axis_index("col")
@@ -180,14 +184,18 @@
         fetches[m].wait()
         fetches[2 + m].wait()
         masked = ins[m][...].astype(F32) * expand(ins[2 + m][...])
-        if m == 1:
-            tm[...] = masked
+        (xm, tm)[m][...] = masked
         padded = tall(masked)
         for j in range(N):
             piece = padded[:, j * ROWS : (j + 1) * ROWS]
             wide = jnp.concatenate([piece, jnp.zeros((PAD, 128 - ROWS), F32)], axis=1)
             a1_send[m, j] = wide.astype(BF16)
-        right0[m, chunk(r), :] = padded.astype(BF16)
+        if m == 1:
+            both = jnp.concatenate([xm[...], masked], axis=0)
+            for u in range(2):
+                pairs[u, r] = both[:, u * 256 : (u + 1) * 256].astype(BF16)
+            last = jnp.concatenate([both[:ROWS, 512:], both[ROWS:, 512:]], axis=1)
+            ends[r] = tall(last).astype(BF16)
         a1_recv[m, d] = a1_send[m, d]
         if m == 0:
             pl.semaphore_wait(barrier, len(greeted))
@@ -220,22 +228,33 @@
         received(lt.at[m, pl.ds(0, NX * PAD), :], c_rs.at[m])
         for i in range(LANES // 128):
             lanes = slice(i * 128, (i + 1) * 128)
-            left[m, lanes, :] = jnp.transpose(lt[m, :, lanes].astype(F32)).astype(BF16)
-
-    def ring(buf, send_sem, recv_sems, m, e, s):
+            panel = lt[m, :, lanes].astype(F32)
+            left[m, lanes, :] = jnp.transpose(panel).astype(BF16)
+            if m == 0:
+                split = panel.reshape(N, PAD, 128)
+                moved = jnp.concatenate([split[:, ROWS:], split[:, :ROWS]], axis=1)
+                left[2, lanes, :] = jnp.transpose(moved.reshape(N * PAD, 128)).astype(BF16)
+
+    def ring(piece_of, send_sem, recv_sems, m, e, s):
         sign, steps = (1, -1)[e], RING_STEPS[m][e]
         at = e * RING_STEPS[m][0]
-        piece = buf.at[m, chunk(wrap(r - sign * s, N)), :]
+        piece = piece_of(wrap(r - sign * s, N))
         if s > 0:
             received(piece, recv_sems.at[at + s - 1])
         if s < steps:
             send(piece, piece, send_sem, recv_sems.at[at + s], at_row(sign))
 
-    def z0(m, e, s):
-        ring(right0, z0_ss.at[m], z0_rs.at[m], m, e, s)
+    def z0(u, e, s):
+        def piece_of(index):
+            return ends.at[index] if u == 2 else pairs.at[u, index]
+
+        ring(piece_of, z0_ss.at[u], z0_rs.at[u], u % 2, e, s)
 
     def z1(h, m, e, s):
-        ring(rights[h], z_ss.at[h, m], z_rs.at[h, m], m, e, s)
+        def piece_of(index):
+            return rights[h].at[m, chunk(index), :]
+
+        ring(piece_of, z_ss.at[h, m], z_rs.at[h, m], m, e, s)
 
     def zt(h, m, q):
         piece = rights[h].at[m, chunk(wrap(r - q, N)), :]
@@ -250,13 +269,25 @@
         steps = (plus, minus)[e]
         part, slot, at = parts[h], slots[h], 7 * k + e * plus
         dest = wrap(d + sign * (steps - s), N)
+        short = SHORT if k == 1 else 0
+        came = None
         if s > 0:
-            received(slot.at[at + s - 1], y_rs.at[h, at + s - 1])
+            piece = shorts[h].at[1, e, s - 1] if s <= short else slot.at[at + s - 1]
+            received(piece, y_rs.at[h, at + s - 1])
             if s < steps:
-                slot[at + s - 1] = slot[at + s - 1] + part[k, dest]
-        if s < steps:
-            source = part.at[k, dest] if s == 0 else slot.at[at + s - 1]
-            send(source, slot.at[at + s], y_ss.at[h], y_rs.at[h, at + s], at_depth(sign))
+                came = piece[...].astype(F32) + part[k, dest]
+        if s == steps:
+            return
+        if s < short:
+            value = part[k, dest] if came is None else came
+            shorts[h][0, e, s] = value.astype(BF16)
+            source, target, done = shorts[h].at[0, e, s], shorts[h].at[1, e, s], b_ss.at[h]
+        else:
+            source, target, done = part.at[k, dest], slot.at[at + s], y_ss.at[h]
+            if came is not None:
+                slot[at + s - 1] = came
+                source = slot.at[at + s - 1]
+        send(source, target, done, y_rs.at[h, at + s], at_depth(sign))
 
     def yt(h, k, stage):
         part, slot, at = parts[h], slots[h], 7 * k
@@ -301,7 +332,7 @@
             rows = pl.ds(pl.multiple_of(i * tile, 16), tile)
             total = None
             for m, right in terms:
-                term = jnp.dot(left[m, rows, :], right[...], preferred_element_type=F32)
+                term = jnp.dot(left[m, rows, :], right(), preferred_element_type=F32)
                 total = term if total is None else total + term
             for b in range(blocks):
                 parts[h][k, i * blocks + b] = pack(total[b * ROWS : (b + 1) * ROWS], h)
@@ -314,8 +345,26 @@
         return slice(start, start + chunk_width(h))
 
     def dot1(h, k):
-        right_x, right_t = (right0.at[m, :, lanes_of(h)] for m in range(2))
-        multiply(h, k, ((0, right_x),) if k == 0 else ((1, right_x), (0, right_t)))
+        tile, tiles, _ = CHUNKS[h]
+
+        def right(m):
+            if tiles == 0:
+                value = ends[:, :, m * 64 : (m + 1) * 64]
+            else:
+                at = (tile % 2) * 128
+                value = pairs[tile // 2, :, m * 64 : m * 64 + PAD, at : at + 128]
+            return value.reshape(N * PAD, value.shape[2])
+
+        def right_x():
+            return right(0)
+
+        def right_t():
+            return right(1)
+
+        if k == 0:
+            multiply(h, k, ((0, right_x),))
+        else:
+            multiply(h, k, ((1, right_x), (0 if tiles == 0 else 2, right_t)))
 
     def sum1(h, k):
         rights[h][k, chunk(r), :] = tall(y_total(h, k)).astype(BF16)
@@ -326,7 +375,7 @@
                 for q in (1, 2, 4, 6, 7):
                     piece = rights[h].at[m, chunk(wrap(r - q, N)), :]
                     received(piece, z_rs.at[h, m, q - 1])
-        multiply(h, 2, ((1, rights[h].at[0]), (0, rights[h].at[1])))
+        multiply(h, 2, ((1, lambda: rights[h][0]), (0, lambda: rights[h][1])))
 
     def fin(h):
         lanes = lanes_of(h)
@@ -342,11 +391,13 @@
     for m in range(2):
         all_sent(a1_send.at[m, pl.ds(0, N - 1)], a1_ss.at[m])
         all_sent(lt.at[m, pl.ds(0, 7 * PAD), :], x_ss.at[m])
-        all_sent(right0.at[m, pl.ds(0, 7 * PAD), :], z0_ss.at[m])
+        all_sent(pairs.at[m, pl.ds(0, N - 1)], z0_ss.at[m])
         for h in range(len(CHUNKS)):
             all_sent(rights[h].at[m, pl.ds(0, 7 * PAD), :], z_ss.at[h, m])
+    all_sent(ends.at[pl.ds(0, N - 1)], z0_ss.at[2])
     for h in range(len(CHUNKS)):
-        all_sent(slots[h], y_ss.at[h])
+        all_sent(slots[h].at[pl.ds(0, 3 * 7 - 2 * SHORT)], y_ss.at[h])
+        all_sent(shorts[h].at[0], b_ss.at[h])
 
 
 def body(x_matrix, tangent, fill_x, fill_t):
@@ -364,18 +415,21 @@
             vmem((2, N, PAD, 128), BF16),
             vmem((2, N, PAD, 128), BF16),
             vmem((2, N * PAD, LANES), BF16),
-            vmem((2, LANES, N * PAD), BF16),
+            vmem((3, LANES, N * PAD), BF16),
             vmem((ROWS, WIDTH), F32),
-            vmem((2, N * PAD, WIDTH), BF16),
+            vmem((ROWS, WIDTH), F32),
+            vmem((2, N, 2 * ROWS, 256), BF16),
+            vmem((N, PAD, 128), BF16),
             *[vmem((2, N * PAD, chunk_width(h)), BF16) for h in range(count)],
             *[vmem((3, N, chunk_rows(h), 128), F32) for h in range(count)],
             *[vmem((3 * 7, chunk_rows(h), 128), F32) for h in range(count)],
+            *[vmem((2, 2, SHORT, chunk_rows(h), 128), BF16) for h in range(count)],
             dma((4,)),
             dma((2,)), dma((2,)),
             dma((2,)), dma((2, 3)), dma((2,)),
-            dma((2,)), dma((2, 7)),
+            dma((3,)), dma((3, 7)),
             dma((count, 2)), dma((count, 2, 7)),
-            dma((count,)), dma((count, 3 * 7)),
+            dma((count,)), dma((count, 3 * 7)), dma((count,)),
         ],
         compiler_params=pltpu.CompilerParams(
             collective_id=0, has_side_effects=True, vmem_limit_bytes=60 * 1024 * 1024

time: 90.7 us -> 88.6 us (0.977)
  Pallas kernels: 88 us -> 86 us
    pallas_call x1, Pallas kernels: 88 us -> 86 us  [body(): pl.pallas_call(kernel, out_shape=jax.ShapeDtypeStruct((ROWS, WIDTH), F32)...]
where the time goes in v3:
time: 88.6 us; the launch traced here: 87.6 us
  Pallas kernels  86 us (97%)
  local copies, waits for them, and re-layouts  1.61 us (2%)
    pallas_call x1, Pallas kernels, body(): pl.pallas_call(kernel, out_shape=jax.ShapeDtypeStruct((ROWS, WIDTH), F32)...  86 us

profile of v3, /device:TPU:6, one launch (start us, length us, event | category | flops | bytes accessed | tf_op | source)
XLA Modules:
  0.0 87.6 jit_solution(7548115858271240127)
XLA Ops:
  0.0 86.0 %shard_map.46 = f32[72,576]{1,0:T(8,128)} custom-call(bf16[72,576]{1,0:T(8,128)(2,1)} %x_hbm.1, bf16[72,576]{1,0:T(8,128)(2,1)} %t_hbm.1, s32[36,36]{1,0:T(8,128)} %fx_hbm.1, s32[36,36]{1,0:T(8,128)} %ft_hbm.1), custom_call_target="tpu_custom_call" | custom-call | tf_op jit(solution)/shard_map/pallas_call | solution.py:408
  86.0 1.6 %copy.6 = f32[72,576]{1,0:T(8,128)} copy(f32[72,576]{1,0:T(8,128)} %shard_map.46) | data formatting | bytes 331776

commit v4 on v3

--- a/solution.py
+++ b/solution.py
@@ -18,59 +18,58 @@
 Z_TREES = ((3, 0), (3, 1), (4, 0), (4, 1))
 Y_TREES = ((4, 2),)
 RING_STEPS = ((4, 3), (3, 4))
-SHORT = 2
 ORDER = (
-    ("prep", 0), ("a1", 0), ("prep", 1), ("z0", 1, 1, 0), ("z0", 2, 0, 0), ("z0", 0, 0, 0), ("a1", 1),
-    ("z0", 0, 1, 0), ("z0", 1, 0, 0), ("z0", 2, 0, 1), ("z0", 1, 1, 1), ("z0", 2, 1, 0), ("z0", 0, 0, 1),
-    ("z0", 2, 0, 2), ("a1f", 0), ("z0", 1, 0, 1), ("z0", 0, 1, 1), ("z0", 1, 1, 2), ("z0", 2, 1, 1),
-    ("z0", 0, 0, 2), ("a1f", 1), ("z0", 0, 1, 2), ("z0", 1, 0, 2), ("z0", 1, 1, 3), ("z0", 2, 0, 3),
-    ("x", 0, 3), ("x", 0, 2), ("z0", 0, 0, 3), ("x", 0, 1), ("z0", 1, 0, 3), ("left", 0), ("x", 1, 2),
-    ("z0", 2, 0, 4), ("x", 1, 1), ("z0", 1, 1, 4), ("dot1", 3, 0), ("y", 3, 0, 1, 0), ("y", 3, 0, 0, 0),
-    ("dot1", 2, 0), ("x", 1, 3), ("z0", 0, 1, 3), ("y", 2, 0, 1, 0), ("y", 2, 0, 0, 0), ("z0", 0, 0, 4),
-    ("dot1", 0, 0), ("dot1", 1, 0), ("y", 0, 0, 0, 0), ("y", 1, 0, 0, 0), ("y", 0, 0, 1, 0),
-    ("y", 1, 0, 1, 0), ("left", 1), ("dot1", 0, 1), ("y", 0, 1, 0, 0), ("z0", 2, 1, 2), ("y", 0, 1, 1, 0),
-    ("y", 3, 0, 0, 1), ("y", 3, 0, 1, 1), ("dot1", 3, 1), ("y", 2, 0, 0, 1), ("y", 3, 1, 0, 0),
-    ("y", 2, 0, 1, 1), ("dot1", 1, 1), ("y", 0, 0, 1, 1), ("y", 1, 1, 1, 0), ("y", 0, 0, 0, 1),
-    ("dot1", 2, 1), ("y", 1, 1, 0, 0), ("y", 0, 1, 1, 1), ("y", 2, 1, 0, 0), ("y", 0, 1, 0, 1),
-    ("y", 2, 1, 1, 0), ("y", 3, 0, 1, 2), ("y", 1, 0, 0, 1), ("y", 1, 0, 1, 1), ("z0", 2, 1, 3),
-    ("y", 2, 0, 1, 2), ("dot1", 4, 1), ("y", 2, 0, 0, 2), ("y", 0, 0, 0, 2), ("y", 0, 1, 1, 2),
-    ("y", 2, 1, 1, 1), ("y", 0, 0, 1, 2), ("y", 3, 1, 1, 0), ("y", 1, 1, 0, 1), ("y", 0, 1, 0, 2),
-    ("dot1", 4, 0), ("y", 3, 1, 0, 1), ("y", 1, 0, 1, 2), ("y", 3, 0, 0, 2), ("y", 2, 0, 0, 3),
-    ("y", 1, 1, 1, 1), ("y", 0, 1, 1, 3), ("y", 0, 0, 0, 3), ("y", 2, 1, 1, 2), ("y", 2, 0, 1, 3),
-    ("y", 2, 1, 0, 1), ("y", 1, 1, 0, 2), ("y", 3, 0, 1, 3), ("y", 4, 1, 1, 0), ("y", 4, 1, 0, 0),
-    ("y", 3, 1, 0, 2), ("y", 4, 0, 0, 0), ("y", 3, 1, 1, 1), ("y", 1, 0, 0, 2), ("y", 1, 1, 1, 2),
-    ("y", 2, 0, 0, 4), ("sum", 2, 0), ("z1", 2, 0, 0, 0), ("y", 0, 0, 1, 3), ("z1", 2, 0, 1, 0),
-    ("y", 0, 1, 0, 3), ("y", 0, 1, 1, 4), ("sum", 0, 1), ("z1", 0, 1, 1, 0), ("y", 0, 0, 0, 4),
-    ("z1", 0, 1, 0, 0), ("sum", 0, 0), ("y", 1, 0, 1, 3), ("z1", 0, 0, 1, 0), ("z1", 0, 0, 0, 0),
-    ("y", 3, 0, 0, 3), ("y", 2, 1, 1, 3), ("y", 2, 1, 0, 2), ("y", 3, 0, 1, 4), ("sum", 3, 0),
-    ("zt", 3, 0, 0), ("y", 1, 1, 0, 3), ("y", 4, 1, 1, 1), ("y", 3, 1, 1, 2), ("y", 3, 1, 0, 3),
-    ("z1", 2, 0, 1, 1), ("z1", 2, 0, 0, 1), ("y", 4, 0, 1, 0), ("y", 1, 1, 1, 3), ("y", 4, 0, 0, 1),
-    ("z1", 0, 1, 1, 1), ("y", 1, 0, 1, 4), ("z1", 0, 1, 0, 1), ("y", 1, 0, 0, 3), ("sum", 1, 0),
-    ("z1", 0, 0, 0, 1), ("z1", 0, 0, 1, 1), ("y", 2, 1, 1, 4), ("y", 2, 1, 0, 3), ("z1", 1, 0, 0, 0),
-    ("sum", 2, 1), ("z1", 2, 1, 1, 0), ("y", 1, 1, 0, 4), ("sum", 1, 1), ("z1", 2, 1, 0, 0),
-    ("z1", 1, 1, 1, 0), ("y", 4, 1, 0, 1), ("z1", 1, 0, 1, 0), ("y", 4, 1, 1, 2), ("y", 3, 1, 1, 3),
-    ("z1", 1, 1, 0, 0), ("y", 3, 1, 0, 4), ("sum", 3, 1), ("zt", 3, 1, 0), ("y", 4, 0, 1, 1),
-    ("z1", 2, 0, 0, 2), ("y", 4, 0, 0, 2), ("z1", 0, 1, 1, 2), ("z1", 1, 0, 0, 1), ("z1", 2, 1, 1, 1),
-    ("z1", 0, 0, 0, 2), ("z1", 2, 1, 0, 1), ("z1", 1, 1, 1, 1), ("y", 4, 0, 1, 2), ("z1", 0, 0, 1, 2),
-    ("z1", 0, 1, 0, 2), ("z1", 1, 1, 0, 1), ("z1", 1, 0, 1, 1), ("zt", 3, 0, 3), ("y", 4, 1, 1, 3),
-    ("y", 4, 1, 0, 2), ("y", 4, 0, 0, 3), ("zt", 3, 0, 5), ("z1", 2, 0, 1, 2), ("z1", 2, 0, 0, 3),
-    ("z1", 0, 1, 1, 3), ("zt", 3, 1, 5), ("z1", 2, 1, 1, 2), ("z1", 1, 0, 0, 2), ("z1", 1, 1, 1, 2),
-    ("zt", 3, 1, 3), ("z1", 0, 0, 0, 3), ("y", 4, 1, 0, 3), ("y", 4, 1, 1, 4), ("z1", 2, 1, 0, 2),
-    ("z1", 1, 0, 1, 2), ("sum", 4, 1), ("z1", 0, 1, 0, 3), ("zt", 4, 1, 0), ("y", 4, 0, 0, 4),
-    ("z1", 0, 0, 1, 3), ("z1", 2, 1, 1, 3), ("y", 4, 0, 1, 3), ("z1", 2, 0, 0, 4), ("z1", 1, 1, 0, 2),
-    ("z1", 1, 1, 1, 3), ("sum", 4, 0), ("z1", 1, 0, 0, 3), ("z1", 0, 1, 1, 4), ("zt", 4, 0, 0), ("dot2", 3),
-    ("y", 3, 2, 0, 0), ("z1", 2, 1, 0, 3), ("z1", 0, 0, 0, 4), ("dot2", 0), ("z1", 1, 0, 1, 3),
-    ("y", 0, 2, 1, 0), ("y", 3, 2, 1, 0), ("y", 0, 2, 0, 0), ("z1", 2, 0, 1, 3), ("z1", 2, 1, 1, 4),
-    ("dot2", 2), ("z1", 1, 1, 1, 4), ("y", 2, 2, 0, 0), ("y", 2, 2, 1, 0), ("zt", 4, 1, 3),
-    ("z1", 1, 1, 0, 3), ("zt", 4, 1, 5), ("z1", 1, 0, 0, 4), ("dot2", 1), ("y", 1, 2, 1, 0),
-    ("y", 3, 2, 0, 1), ("y", 0, 2, 1, 1), ("y", 1, 2, 0, 0), ("y", 0, 2, 0, 1), ("zt", 4, 0, 5),
-    ("y", 3, 2, 1, 1), ("zt", 4, 0, 3), ("y", 2, 2, 0, 1), ("y", 2, 2, 1, 1), ("y", 3, 2, 0, 2),
-    ("y", 1, 2, 1, 1), ("y", 0, 2, 1, 2), ("y", 1, 2, 0, 1), ("y", 3, 2, 1, 2), ("y", 0, 2, 0, 2),
-    ("dot2", 4), ("yt", 4, 2, 0), ("y", 2, 2, 0, 2), ("y", 1, 2, 1, 2), ("y", 3, 2, 0, 3),
-    ("y", 2, 2, 1, 2), ("y", 1, 2, 0, 2), ("y", 3, 2, 1, 3), ("yt", 4, 2, 1), ("y", 0, 2, 0, 3),
-    ("yt", 4, 2, 2), ("y", 1, 2, 1, 3), ("y", 2, 2, 0, 3), ("y", 2, 2, 1, 3), ("y", 3, 2, 1, 4),
-    ("y", 0, 2, 1, 3), ("y", 0, 2, 0, 4), ("fin", 0), ("fin", 3), ("y", 1, 2, 1, 4), ("y", 1, 2, 0, 3),
-    ("fin", 1), ("y", 2, 2, 0, 4), ("fin", 2), ("fin", 4),
+    ("prep", 0), ("a1", 0), ("prep", 1), ("z0", 2, 0, 0), ("z0", 1, 1, 0), ("a1", 1), ("z0", 0, 0, 0),
+    ("z0", 0, 1, 0), ("z0", 2, 1, 0), ("z0", 1, 0, 0), ("z0", 2, 0, 1), ("z0", 1, 1, 1), ("z0", 0, 0, 1),
+    ("z0", 0, 1, 1), ("a1f", 0), ("z0", 1, 0, 1), ("z0", 2, 0, 2), ("z0", 1, 1, 2), ("z0", 2, 1, 1),
+    ("z0", 0, 0, 2), ("a1f", 1), ("z0", 1, 0, 2), ("z0", 0, 1, 2), ("x", 0, 3), ("z0", 1, 1, 3),
+    ("z0", 2, 1, 2), ("z0", 0, 0, 3), ("x", 0, 2), ("z0", 2, 0, 3), ("z0", 1, 0, 3), ("x", 0, 1),
+    ("z0", 0, 1, 3), ("left", 0), ("z0", 1, 1, 4), ("dot1", 2, 0), ("y", 2, 0, 1, 0), ("z0", 0, 0, 4),
+    ("y", 2, 0, 0, 0), ("x", 1, 1), ("dot1", 1, 0), ("y", 1, 0, 1, 0), ("y", 1, 0, 0, 0), ("dot1", 0, 0),
+    ("dot1", 3, 0), ("z0", 2, 1, 3), ("y", 0, 0, 1, 0), ("y", 3, 0, 1, 0), ("y", 0, 0, 0, 0), ("x", 1, 2),
+    ("x", 1, 3), ("y", 3, 0, 0, 0), ("y", 2, 0, 1, 1), ("y", 2, 0, 0, 1), ("left", 1), ("y", 1, 0, 1, 1),
+    ("y", 1, 0, 0, 1), ("dot1", 0, 1), ("y", 0, 1, 0, 0), ("y", 0, 0, 0, 1), ("y", 0, 1, 1, 0),
+    ("dot1", 2, 1), ("y", 2, 1, 1, 0), ("y", 2, 1, 0, 0), ("y", 0, 0, 1, 1), ("dot1", 1, 1),
+    ("y", 2, 0, 0, 2), ("y", 1, 1, 0, 0), ("y", 1, 0, 1, 2), ("y", 1, 1, 1, 0), ("dot1", 3, 1),
+    ("y", 1, 0, 0, 2), ("y", 0, 1, 1, 1), ("y", 0, 0, 0, 2), ("y", 2, 1, 1, 1), ("y", 3, 1, 0, 0),
+    ("y", 2, 0, 1, 2), ("z0", 2, 0, 4), ("y", 2, 0, 0, 3), ("y", 1, 0, 1, 3), ("y", 0, 0, 1, 2),
+    ("dot1", 4, 0), ("y", 3, 1, 1, 0), ("y", 1, 1, 0, 1), ("y", 2, 1, 0, 1), ("y", 0, 0, 0, 3),
+    ("dot1", 4, 1), ("y", 2, 1, 1, 2), ("y", 1, 0, 0, 3), ("y", 3, 1, 0, 1), ("y", 0, 1, 1, 2),
+    ("y", 2, 0, 1, 3), ("y", 0, 1, 0, 1), ("y", 1, 0, 1, 4), ("sum", 1, 0), ("z1", 1, 0, 0, 0),
+    ("y", 1, 1, 1, 1), ("y", 2, 0, 0, 4), ("z1", 1, 0, 1, 0), ("y", 3, 0, 1, 1), ("sum", 2, 0),
+    ("y", 1, 1, 0, 2), ("y", 0, 0, 1, 3), ("y", 4, 0, 0, 0), ("z1", 2, 0, 1, 0), ("z1", 2, 0, 0, 0),
+    ("y", 4, 0, 1, 0), ("y", 2, 1, 0, 2), ("y", 0, 0, 0, 4), ("sum", 0, 0), ("z1", 0, 0, 1, 0),
+    ("y", 2, 1, 1, 3), ("z1", 0, 0, 0, 0), ("y", 3, 1, 1, 1), ("y", 3, 1, 0, 2), ("z1", 1, 0, 1, 1),
+    ("z1", 1, 0, 0, 1), ("y", 0, 1, 1, 3), ("y", 0, 1, 0, 2), ("y", 1, 1, 1, 2), ("z1", 2, 0, 1, 1),
+    ("z1", 2, 0, 0, 1), ("y", 1, 1, 0, 3), ("y", 3, 0, 0, 1), ("y", 3, 0, 1, 2), ("y", 2, 1, 0, 3),
+    ("z1", 0, 0, 0, 1), ("y", 2, 1, 1, 4), ("sum", 2, 1), ("z1", 2, 1, 0, 0), ("z1", 2, 1, 1, 0),
+    ("y", 4, 0, 0, 1), ("z1", 0, 0, 1, 1), ("y", 3, 1, 0, 3), ("y", 3, 1, 1, 2), ("z1", 1, 0, 0, 2),
+    ("y", 0, 1, 0, 3), ("z1", 1, 0, 1, 2), ("y", 0, 1, 1, 4), ("sum", 0, 1), ("y", 4, 1, 1, 0),
+    ("z1", 0, 1, 0, 0), ("z1", 2, 0, 0, 2), ("z1", 2, 0, 1, 2), ("y", 4, 1, 0, 0), ("z1", 0, 1, 1, 0),
+    ("y", 1, 1, 1, 3), ("y", 1, 1, 0, 4), ("y", 4, 0, 1, 1), ("sum", 1, 1), ("z1", 1, 1, 0, 0),
+    ("z1", 1, 1, 1, 0), ("z1", 0, 0, 0, 2), ("y", 3, 0, 0, 2), ("z1", 2, 1, 1, 1), ("y", 3, 0, 1, 3),
+    ("z1", 2, 1, 0, 1), ("z1", 0, 0, 1, 2), ("y", 4, 0, 0, 2), ("z1", 1, 0, 0, 3), ("y", 3, 1, 0, 4),
+    ("y", 3, 1, 1, 3), ("sum", 3, 1), ("zt", 3, 1, 0), ("y", 4, 1, 1, 1), ("z1", 1, 1, 1, 1),
+    ("y", 4, 1, 0, 1), ("z1", 1, 0, 1, 3), ("z1", 0, 1, 1, 1), ("z1", 1, 1, 0, 1), ("z1", 0, 1, 0, 1),
+    ("y", 4, 0, 1, 2), ("y", 3, 0, 1, 4), ("y", 3, 0, 0, 3), ("z1", 2, 1, 1, 2), ("sum", 3, 0),
+    ("z1", 2, 0, 0, 3), ("y", 4, 0, 0, 3), ("z1", 2, 0, 1, 3), ("z1", 0, 0, 0, 3), ("z1", 1, 0, 0, 4),
+    ("zt", 3, 0, 0), ("z1", 2, 1, 0, 2), ("y", 4, 1, 1, 2), ("z1", 1, 1, 1, 2), ("y", 4, 0, 1, 3),
+    ("z1", 0, 1, 1, 2), ("z1", 1, 1, 0, 2), ("y", 4, 0, 0, 4), ("z1", 2, 1, 1, 3), ("z1", 0, 1, 0, 2),
+    ("sum", 4, 0), ("y", 4, 1, 0, 2), ("zt", 4, 0, 0), ("y", 4, 1, 1, 3), ("z1", 1, 1, 1, 3),
+    ("zt", 3, 1, 3), ("z1", 0, 1, 1, 3), ("zt", 3, 1, 5), ("zt", 3, 0, 5), ("z1", 2, 1, 1, 4),
+    ("zt", 3, 0, 3), ("y", 4, 1, 0, 3), ("y", 4, 1, 1, 4), ("z1", 0, 0, 1, 3), ("z1", 2, 0, 0, 4),
+    ("sum", 4, 1), ("zt", 4, 1, 0), ("z1", 1, 1, 0, 3), ("z1", 2, 1, 0, 3), ("dot2", 2), ("z1", 1, 1, 1, 4),
+    ("z1", 0, 1, 0, 3), ("y", 2, 2, 0, 0), ("z1", 0, 0, 0, 4), ("y", 2, 2, 1, 0), ("dot2", 1),
+    ("y", 1, 2, 1, 0), ("zt", 4, 0, 5), ("z1", 0, 1, 1, 4), ("y", 1, 2, 0, 0), ("dot2", 0),
+    ("y", 0, 2, 1, 0), ("zt", 4, 0, 3), ("y", 0, 2, 0, 0), ("dot2", 3), ("y", 3, 2, 0, 0),
+    ("y", 3, 2, 1, 0), ("y", 2, 2, 0, 1), ("y", 2, 2, 1, 1), ("zt", 4, 1, 5), ("zt", 4, 1, 3),
+    ("y", 1, 2, 1, 1), ("y", 1, 2, 0, 1), ("y", 0, 2, 0, 1), ("y", 0, 2, 1, 1), ("y", 3, 2, 1, 1),
+    ("y", 3, 2, 0, 1), ("y", 2, 2, 0, 2), ("y", 2, 2, 1, 2), ("dot2", 4), ("yt", 4, 2, 0),
+    ("y", 0, 2, 0, 2), ("y", 1, 2, 1, 2), ("y", 3, 2, 1, 2), ("y", 1, 2, 0, 2), ("y", 0, 2, 1, 2),
+    ("y", 2, 2, 1, 3), ("y", 2, 2, 0, 3), ("yt", 4, 2, 1), ("yt", 4, 2, 2), ("y", 1, 2, 1, 3),
+    ("y", 0, 2, 0, 3), ("y", 3, 2, 0, 2), ("y", 1, 2, 0, 3), ("y", 3, 2, 1, 3), ("y", 0, 2, 1, 3),
+    ("y", 0, 2, 0, 4), ("y", 2, 2, 0, 4), ("fin", 2), ("fin", 0), ("fin", 4), ("y", 1, 2, 1, 4), ("fin", 1),
+    ("y", 3, 2, 1, 4), ("y", 3, 2, 0, 3), ("fin", 3),
 )
 
 
@@ -110,8 +109,7 @@
     rights = [scratch.pop(0) for _ in CHUNKS]
     parts = [scratch.pop(0) for _ in CHUNKS]
     slots = [scratch.pop(0) for _ in CHUNKS]
-    shorts = [scratch.pop(0) for _ in CHUNKS]
-    in_s, a1_ss, a1_rs, x_ss, x_rs, c_rs, z0_ss, z0_rs, z_ss, z_rs, y_ss, y_rs, b_ss = scratch
+    in_s, a1_ss, a1_rs, x_ss, x_rs, c_rs, z0_ss, z0_rs, z_ss, z_rs, y_ss, y_rs = scratch
 
     r = lax.axis_index("row")
     c = lax.axis_index("col")
@@ -269,25 +267,13 @@
         steps = (plus, minus)[e]
         part, slot, at = parts[h], slots[h], 7 * k + e * plus
         dest = wrap(d + sign * (steps - s), N)
-        short = SHORT if k == 1 else 0
-        came = None
         if s > 0:
-            piece = shorts[h].at[1, e, s - 1] if s <= short else slot.at[at + s - 1]
-            received(piece, y_rs.at[h, at + s - 1])
+            received(slot.at[at + s - 1], y_rs.at[h, at + s - 1])
             if s < steps:
-                came = piece[...].astype(F32) + part[k, dest]
-        if s == steps:
-            return
-        if s < short:
-            value = part[k, dest] if came is None else came
-            shorts[h][0, e, s] = value.astype(BF16)
-            source, target, done = shorts[h].at[0, e, s], shorts[h].at[1, e, s], b_ss.at[h]
-        else:
-            source, target, done = part.at[k, dest], slot.at[at + s], y_ss.at[h]
-            if came is not None:
-                slot[at + s - 1] = came
-                source = slot.at[at + s - 1]
-        send(source, target, done, y_rs.at[h, at + s], at_depth(sign))
+                slot[at + s - 1] = slot[at + s - 1] + part[k, dest]
+        if s < steps:
+            source = part.at[k, dest] if s == 0 else slot.at[at + s - 1]
+            send(source, slot.at[at + s], y_ss.at[h], y_rs.at[h, at + s], at_depth(sign))
 
     def yt(h, k, stage):
         part, slot, at = parts[h], slots[h], 7 * k
@@ -396,8 +382,7 @@
             all_sent(rights[h].at[m, pl.ds(0, 7 * PAD), :], z_ss.at[h, m])
     all_sent(ends.at[pl.ds(0, N - 1)], z0_ss.at[2])
     for h in range(len(CHUNKS)):
-        all_sent(slots[h].at[pl.ds(0, 3 * 7 - 2 * SHORT)], y_ss.at[h])
-        all_sent(shorts[h].at[0], b_ss.at[h])
+        all_sent(slots[h], y_ss.at[h])
 
 
 def body(x_matrix, tangent, fill_x, fill_t):
@@ -423,13 +408,12 @@
             *[vmem((2, N * PAD, chunk_width(h)), BF16) for h in range(count)],
             *[vmem((3, N, chunk_rows(h), 128), F32) for h in range(count)],
             *[vmem((3 * 7, chunk_rows(h), 128), F32) for h in range(count)],
-            *[vmem((2, 2, SHORT, chunk_rows(h), 128), BF16) for h in range(count)],
             dma((4,)),
             dma((2,)), dma((2,)),
             dma((2,)), dma((2, 3)), dma((2,)),
             dma((3,)), dma((3, 7)),
             dma((count, 2)), dma((count, 2, 7)),
-            dma((count,)), dma((count, 3 * 7)), dma((count,)),
+            dma((count,)), dma((count, 3 * 7)),
         ],
         compiler_params=pltpu.CompilerParams(
             collective_id=0, has_side_effects=True, vmem_limit_bytes=60 * 1024 * 1024

time: 88.6 us -> 89.9 us (1.015)
  Pallas kernels: 86 us -> 87.9 us
    pallas_call x1, Pallas kernels: 86 us -> 87.9 us  [body(): pl.pallas_call(kernel, out_shape=jax.ShapeDtypeStruct((ROWS, WIDTH), F32)...]
where the time goes in v4:
time: 89.9 us; the launch traced here: 89.5 us
  Pallas kernels  87.9 us (98%)
  local copies, waits for them, and re-layouts  1.61 us (2%)
    pallas_call x1, Pallas kernels, body(): pl.pallas_call(kernel, out_shape=jax.ShapeDtypeStruct((ROWS, WIDTH), F32)...  87.9 us

profile of v4, /device:TPU:6, one launch (start us, length us, event | category | flops | bytes accessed | tf_op | source)
XLA Modules:
  0.0 89.5 jit_solution(14996101040054711825)
XLA Ops:
  0.0 87.9 %shard_map.46 = f32[72,576]{1,0:T(8,128)} custom-call(bf16[72,576]{1,0:T(8,128)(2,1)} %x_hbm.1, bf16[72,576]{1,0:T(8,128)(2,1)} %t_hbm.1, s32[36,36]{1,0:T(8,128)} %fx_hbm.1, s32[36,36]{1,0:T(8,128)} %ft_hbm.1), custom_call_target="tpu_custom_call" | custom-call | tf_op jit(solution)/shard_map/pallas_call | solution.py:393
  87.9 1.6 %copy.6 = f32[72,576]{1,0:T(8,128)} copy(f32[72,576]{1,0:T(8,128)} %shard_map.46) | data formatting | bytes 331776

commit v5 on v3

--- a/solution.py
+++ b/solution.py
@@ -20,57 +20,57 @@
 RING_STEPS = ((4, 3), (3, 4))
 SHORT = 2
 ORDER = (
-    ("prep", 0), ("a1", 0), ("prep", 1), ("z0", 1, 1, 0), ("z0", 2, 0, 0), ("z0", 0, 0, 0), ("a1", 1),
-    ("z0", 0, 1, 0), ("z0", 1, 0, 0), ("z0", 2, 0, 1), ("z0", 1, 1, 1), ("z0", 2, 1, 0), ("z0", 0, 0, 1),
-    ("z0", 2, 0, 2), ("a1f", 0), ("z0", 1, 0, 1), ("z0", 0, 1, 1), ("z0", 1, 1, 2), ("z0", 2, 1, 1),
-    ("z0", 0, 0, 2), ("a1f", 1), ("z0", 0, 1, 2), ("z0", 1, 0, 2), ("z0", 1, 1, 3), ("z0", 2, 0, 3),
-    ("x", 0, 3), ("x", 0, 2), ("z0", 0, 0, 3), ("x", 0, 1), ("z0", 1, 0, 3), ("left", 0), ("x", 1, 2),
-    ("z0", 2, 0, 4), ("x", 1, 1), ("z0", 1, 1, 4), ("dot1", 3, 0), ("y", 3, 0, 1, 0), ("y", 3, 0, 0, 0),
-    ("dot1", 2, 0), ("x", 1, 3), ("z0", 0, 1, 3), ("y", 2, 0, 1, 0), ("y", 2, 0, 0, 0), ("z0", 0, 0, 4),
-    ("dot1", 0, 0), ("dot1", 1, 0), ("y", 0, 0, 0, 0), ("y", 1, 0, 0, 0), ("y", 0, 0, 1, 0),
-    ("y", 1, 0, 1, 0), ("left", 1), ("dot1", 0, 1), ("y", 0, 1, 0, 0), ("z0", 2, 1, 2), ("y", 0, 1, 1, 0),
-    ("y", 3, 0, 0, 1), ("y", 3, 0, 1, 1), ("dot1", 3, 1), ("y", 2, 0, 0, 1), ("y", 3, 1, 0, 0),
-    ("y", 2, 0, 1, 1), ("dot1", 1, 1), ("y", 0, 0, 1, 1), ("y", 1, 1, 1, 0), ("y", 0, 0, 0, 1),
-    ("dot1", 2, 1), ("y", 1, 1, 0, 0), ("y", 0, 1, 1, 1), ("y", 2, 1, 0, 0), ("y", 0, 1, 0, 1),
-    ("y", 2, 1, 1, 0), ("y", 3, 0, 1, 2), ("y", 1, 0, 0, 1), ("y", 1, 0, 1, 1), ("z0", 2, 1, 3),
-    ("y", 2, 0, 1, 2), ("dot1", 4, 1), ("y", 2, 0, 0, 2), ("y", 0, 0, 0, 2), ("y", 0, 1, 1, 2),
-    ("y", 2, 1, 1, 1), ("y", 0, 0, 1, 2), ("y", 3, 1, 1, 0), ("y", 1, 1, 0, 1), ("y", 0, 1, 0, 2),
-    ("dot1", 4, 0), ("y", 3, 1, 0, 1), ("y", 1, 0, 1, 2), ("y", 3, 0, 0, 2), ("y", 2, 0, 0, 3),
-    ("y", 1, 1, 1, 1), ("y", 0, 1, 1, 3), ("y", 0, 0, 0, 3), ("y", 2, 1, 1, 2), ("y", 2, 0, 1, 3),
-    ("y", 2, 1, 0, 1), ("y", 1, 1, 0, 2), ("y", 3, 0, 1, 3), ("y", 4, 1, 1, 0), ("y", 4, 1, 0, 0),
-    ("y", 3, 1, 0, 2), ("y", 4, 0, 0, 0), ("y", 3, 1, 1, 1), ("y", 1, 0, 0, 2), ("y", 1, 1, 1, 2),
-    ("y", 2, 0, 0, 4), ("sum", 2, 0), ("z1", 2, 0, 0, 0), ("y", 0, 0, 1, 3), ("z1", 2, 0, 1, 0),
-    ("y", 0, 1, 0, 3), ("y", 0, 1, 1, 4), ("sum", 0, 1), ("z1", 0, 1, 1, 0), ("y", 0, 0, 0, 4),
-    ("z1", 0, 1, 0, 0), ("sum", 0, 0), ("y", 1, 0, 1, 3), ("z1", 0, 0, 1, 0), ("z1", 0, 0, 0, 0),
-    ("y", 3, 0, 0, 3), ("y", 2, 1, 1, 3), ("y", 2, 1, 0, 2), ("y", 3, 0, 1, 4), ("sum", 3, 0),
-    ("zt", 3, 0, 0), ("y", 1, 1, 0, 3), ("y", 4, 1, 1, 1), ("y", 3, 1, 1, 2), ("y", 3, 1, 0, 3),
-    ("z1", 2, 0, 1, 1), ("z1", 2, 0, 0, 1), ("y", 4, 0, 1, 0), ("y", 1, 1, 1, 3), ("y", 4, 0, 0, 1),
-    ("z1", 0, 1, 1, 1), ("y", 1, 0, 1, 4), ("z1", 0, 1, 0, 1), ("y", 1, 0, 0, 3), ("sum", 1, 0),
-    ("z1", 0, 0, 0, 1), ("z1", 0, 0, 1, 1), ("y", 2, 1, 1, 4), ("y", 2, 1, 0, 3), ("z1", 1, 0, 0, 0),
-    ("sum", 2, 1), ("z1", 2, 1, 1, 0), ("y", 1, 1, 0, 4), ("sum", 1, 1), ("z1", 2, 1, 0, 0),
-    ("z1", 1, 1, 1, 0), ("y", 4, 1, 0, 1), ("z1", 1, 0, 1, 0), ("y", 4, 1, 1, 2), ("y", 3, 1, 1, 3),
-    ("z1", 1, 1, 0, 0), ("y", 3, 1, 0, 4), ("sum", 3, 1), ("zt", 3, 1, 0), ("y", 4, 0, 1, 1),
-    ("z1", 2, 0, 0, 2), ("y", 4, 0, 0, 2), ("z1", 0, 1, 1, 2), ("z1", 1, 0, 0, 1), ("z1", 2, 1, 1, 1),
-    ("z1", 0, 0, 0, 2), ("z1", 2, 1, 0, 1), ("z1", 1, 1, 1, 1), ("y", 4, 0, 1, 2), ("z1", 0, 0, 1, 2),
-    ("z1", 0, 1, 0, 2), ("z1", 1, 1, 0, 1), ("z1", 1, 0, 1, 1), ("zt", 3, 0, 3), ("y", 4, 1, 1, 3),
-    ("y", 4, 1, 0, 2), ("y", 4, 0, 0, 3), ("zt", 3, 0, 5), ("z1", 2, 0, 1, 2), ("z1", 2, 0, 0, 3),
-    ("z1", 0, 1, 1, 3), ("zt", 3, 1, 5), ("z1", 2, 1, 1, 2), ("z1", 1, 0, 0, 2), ("z1", 1, 1, 1, 2),
-    ("zt", 3, 1, 3), ("z1", 0, 0, 0, 3), ("y", 4, 1, 0, 3), ("y", 4, 1, 1, 4), ("z1", 2, 1, 0, 2),
-    ("z1", 1, 0, 1, 2), ("sum", 4, 1), ("z1", 0, 1, 0, 3), ("zt", 4, 1, 0), ("y", 4, 0, 0, 4),
-    ("z1", 0, 0, 1, 3), ("z1", 2, 1, 1, 3), ("y", 4, 0, 1, 3), ("z1", 2, 0, 0, 4), ("z1", 1, 1, 0, 2),
-    ("z1", 1, 1, 1, 3), ("sum", 4, 0), ("z1", 1, 0, 0, 3), ("z1", 0, 1, 1, 4), ("zt", 4, 0, 0), ("dot2", 3),
-    ("y", 3, 2, 0, 0), ("z1", 2, 1, 0, 3), ("z1", 0, 0, 0, 4), ("dot2", 0), ("z1", 1, 0, 1, 3),
-    ("y", 0, 2, 1, 0), ("y", 3, 2, 1, 0), ("y", 0, 2, 0, 0), ("z1", 2, 0, 1, 3), ("z1", 2, 1, 1, 4),
-    ("dot2", 2), ("z1", 1, 1, 1, 4), ("y", 2, 2, 0, 0), ("y", 2, 2, 1, 0), ("zt", 4, 1, 3),
-    ("z1", 1, 1, 0, 3), ("zt", 4, 1, 5), ("z1", 1, 0, 0, 4), ("dot2", 1), ("y", 1, 2, 1, 0),
-    ("y", 3, 2, 0, 1), ("y", 0, 2, 1, 1), ("y", 1, 2, 0, 0), ("y", 0, 2, 0, 1), ("zt", 4, 0, 5),
-    ("y", 3, 2, 1, 1), ("zt", 4, 0, 3), ("y", 2, 2, 0, 1), ("y", 2, 2, 1, 1), ("y", 3, 2, 0, 2),
-    ("y", 1, 2, 1, 1), ("y", 0, 2, 1, 2), ("y", 1, 2, 0, 1), ("y", 3, 2, 1, 2), ("y", 0, 2, 0, 2),
-    ("dot2", 4), ("yt", 4, 2, 0), ("y", 2, 2, 0, 2), ("y", 1, 2, 1, 2), ("y", 3, 2, 0, 3),
-    ("y", 2, 2, 1, 2), ("y", 1, 2, 0, 2), ("y", 3, 2, 1, 3), ("yt", 4, 2, 1), ("y", 0, 2, 0, 3),
-    ("yt", 4, 2, 2), ("y", 1, 2, 1, 3), ("y", 2, 2, 0, 3), ("y", 2, 2, 1, 3), ("y", 3, 2, 1, 4),
-    ("y", 0, 2, 1, 3), ("y", 0, 2, 0, 4), ("fin", 0), ("fin", 3), ("y", 1, 2, 1, 4), ("y", 1, 2, 0, 3),
-    ("fin", 1), ("y", 2, 2, 0, 4), ("fin", 2), ("fin", 4),
+    ("prep", 0), ("a1", 0), ("prep", 1), ("z0", 0, 0, 0), ("z0", 1, 1, 0), ("z0", 0, 1, 0), ("z0", 1, 0, 0),
+    ("a1", 1), ("z0", 2, 1, 0), ("z0", 2, 0, 0), ("z0", 0, 0, 1), ("z0", 1, 1, 1), ("z0", 0, 1, 1),
+    ("z0", 1, 0, 1), ("a1f", 0), ("z0", 2, 1, 1), ("z0", 0, 0, 2), ("z0", 1, 1, 2), ("z0", 0, 1, 2),
+    ("z0", 1, 0, 2), ("a1f", 1), ("z0", 2, 1, 2), ("z0", 0, 0, 3), ("z0", 1, 1, 3), ("z0", 0, 1, 3),
+    ("z0", 2, 0, 1), ("x", 0, 2), ("z0", 1, 0, 3), ("x", 0, 3), ("x", 0, 1), ("z0", 2, 1, 3), ("left", 0),
+    ("z0", 1, 1, 4), ("dot1", 2, 0), ("y", 2, 0, 1, 0), ("y", 2, 0, 0, 0), ("z0", 2, 0, 2), ("dot1", 3, 0),
+    ("x", 1, 1), ("z0", 0, 0, 4), ("y", 3, 0, 1, 0), ("x", 1, 2), ("y", 3, 0, 0, 0), ("dot1", 0, 0),
+    ("y", 0, 0, 0, 0), ("y", 0, 0, 1, 0), ("x", 1, 3), ("dot1", 1, 0), ("y", 1, 0, 0, 0), ("y", 1, 0, 1, 0),
+    ("z0", 2, 0, 3), ("y", 2, 0, 1, 1), ("y", 2, 0, 0, 1), ("left", 1), ("y", 3, 0, 1, 1),
+    ("y", 3, 0, 0, 1), ("dot1", 2, 1), ("y", 2, 1, 1, 0), ("y", 2, 1, 0, 0), ("y", 0, 0, 0, 1),
+    ("y", 0, 0, 1, 1), ("dot1", 1, 1), ("y", 1, 0, 1, 1), ("y", 1, 0, 0, 1), ("y", 1, 1, 1, 0),
+    ("y", 1, 1, 0, 0), ("z0", 2, 0, 4), ("dot1", 0, 1), ("y", 0, 1, 1, 0), ("y", 0, 1, 0, 0),
+    ("y", 2, 0, 0, 2), ("y", 3, 0, 1, 2), ("dot1", 3, 1), ("y", 2, 1, 1, 1), ("y", 2, 0, 1, 2),
+    ("y", 3, 1, 0, 0), ("y", 3, 0, 0, 2), ("dot1", 4, 1), ("dot1", 4, 0), ("y", 1, 0, 1, 2),
+    ("y", 1, 0, 0, 2), ("y", 0, 1, 1, 1), ("y", 1, 1, 0, 1), ("y", 3, 1, 1, 0), ("y", 2, 1, 0, 1),
+    ("y", 2, 0, 0, 3), ("y", 3, 0, 1, 3), ("y", 2, 1, 1, 2), ("y", 3, 1, 0, 1), ("y", 0, 0, 0, 2),
+    ("y", 0, 1, 0, 1), ("y", 1, 0, 1, 3), ("y", 3, 0, 0, 3), ("y", 1, 0, 0, 3), ("y", 1, 1, 0, 2),
+    ("y", 0, 1, 1, 2), ("y", 1, 1, 1, 1), ("y", 3, 1, 1, 1), ("y", 2, 0, 1, 3), ("y", 2, 1, 0, 2),
+    ("y", 3, 0, 1, 4), ("y", 2, 0, 0, 4), ("sum", 2, 0), ("z1", 2, 0, 0, 0), ("z1", 2, 0, 1, 0),
+    ("sum", 3, 0), ("zt", 3, 0, 0), ("y", 3, 1, 0, 2), ("y", 2, 1, 1, 3), ("y", 0, 0, 1, 2),
+    ("y", 0, 0, 0, 3), ("y", 1, 0, 1, 4), ("y", 4, 0, 0, 0), ("y", 4, 1, 1, 0), ("y", 0, 1, 0, 2),
+    ("sum", 1, 0), ("z1", 1, 0, 1, 0), ("z1", 1, 0, 0, 0), ("y", 0, 1, 1, 3), ("y", 1, 1, 0, 3),
+    ("y", 2, 1, 0, 3), ("y", 1, 1, 1, 2), ("z1", 2, 0, 0, 1), ("y", 3, 1, 1, 2), ("z1", 2, 0, 1, 1),
+    ("y", 3, 1, 0, 3), ("y", 2, 1, 1, 4), ("sum", 2, 1), ("z1", 2, 1, 1, 0), ("z1", 2, 1, 0, 0),
+    ("y", 0, 0, 0, 4), ("y", 4, 0, 1, 0), ("y", 0, 0, 1, 3), ("sum", 0, 0), ("z1", 0, 0, 0, 0),
+    ("y", 4, 0, 0, 1), ("y", 4, 1, 1, 1), ("y", 4, 1, 0, 0), ("z1", 1, 0, 0, 1), ("z1", 0, 0, 1, 0),
+    ("z1", 1, 0, 1, 1), ("y", 0, 1, 0, 3), ("zt", 3, 0, 5), ("y", 0, 1, 1, 4), ("sum", 0, 1),
+    ("z1", 0, 1, 1, 0), ("z1", 0, 1, 0, 0), ("z1", 2, 0, 0, 2), ("y", 1, 1, 1, 3), ("y", 1, 1, 0, 4),
+    ("sum", 1, 1), ("z1", 1, 1, 1, 0), ("z1", 1, 1, 0, 0), ("z1", 2, 1, 1, 1), ("z1", 2, 1, 0, 1),
+    ("y", 3, 1, 1, 3), ("y", 3, 1, 0, 4), ("sum", 3, 1), ("zt", 3, 1, 0), ("y", 4, 0, 0, 2),
+    ("y", 4, 0, 1, 1), ("z1", 0, 1, 1, 1), ("y", 4, 1, 1, 2), ("z1", 0, 0, 0, 1), ("y", 4, 1, 0, 1),
+    ("z1", 1, 0, 0, 2), ("z1", 1, 1, 1, 1), ("z1", 2, 1, 1, 2), ("z1", 1, 1, 0, 1), ("z1", 0, 0, 1, 1),
+    ("z1", 2, 0, 1, 2), ("z1", 2, 0, 0, 3), ("z1", 0, 1, 0, 1), ("y", 4, 0, 0, 3), ("zt", 3, 0, 3),
+    ("y", 4, 0, 1, 2), ("z1", 2, 1, 0, 2), ("z1", 1, 0, 1, 2), ("z1", 0, 1, 1, 2), ("y", 4, 1, 1, 3),
+    ("zt", 3, 1, 5), ("z1", 1, 1, 1, 2), ("y", 4, 1, 0, 2), ("z1", 0, 0, 0, 2), ("zt", 3, 1, 3),
+    ("z1", 2, 1, 1, 3), ("y", 4, 0, 0, 4), ("z1", 0, 0, 1, 2), ("z1", 1, 1, 0, 2), ("y", 4, 0, 1, 3),
+    ("z1", 1, 0, 0, 3), ("z1", 2, 0, 1, 3), ("sum", 4, 0), ("zt", 4, 0, 0), ("z1", 2, 1, 0, 3),
+    ("y", 4, 1, 1, 4), ("y", 4, 1, 0, 3), ("z1", 1, 1, 1, 3), ("z1", 0, 0, 0, 3), ("z1", 2, 0, 0, 4),
+    ("sum", 4, 1), ("z1", 0, 1, 0, 2), ("z1", 0, 1, 1, 3), ("zt", 4, 1, 0), ("dot2", 3), ("z1", 2, 1, 1, 4),
+    ("dot2", 2), ("y", 2, 2, 0, 0), ("y", 3, 2, 0, 0), ("y", 3, 2, 1, 0), ("z1", 1, 0, 1, 3),
+    ("y", 2, 2, 1, 0), ("z1", 1, 1, 0, 3), ("z1", 1, 0, 0, 4), ("z1", 1, 1, 1, 4), ("dot2", 1),
+    ("z1", 0, 0, 0, 4), ("zt", 4, 0, 3), ("z1", 0, 0, 1, 3), ("z1", 0, 1, 1, 4), ("zt", 4, 0, 5),
+    ("y", 1, 2, 0, 0), ("z1", 0, 1, 0, 3), ("y", 1, 2, 1, 0), ("dot2", 0), ("y", 0, 2, 1, 0),
+    ("y", 0, 2, 0, 0), ("y", 3, 2, 1, 1), ("y", 2, 2, 0, 1), ("zt", 4, 1, 5), ("y", 3, 2, 0, 1),
+    ("zt", 4, 1, 3), ("y", 2, 2, 1, 1), ("y", 1, 2, 1, 1), ("y", 1, 2, 0, 1), ("y", 0, 2, 0, 1),
+    ("y", 0, 2, 1, 1), ("y", 2, 2, 0, 2), ("y", 3, 2, 1, 2), ("dot2", 4), ("yt", 4, 2, 0),
+    ("y", 1, 2, 1, 2), ("y", 1, 2, 0, 2), ("y", 2, 2, 1, 2), ("y", 0, 2, 0, 2), ("y", 3, 2, 0, 2),
+    ("y", 3, 2, 1, 3), ("yt", 4, 2, 1), ("yt", 4, 2, 2), ("y", 1, 2, 1, 3), ("y", 0, 2, 1, 2),
+    ("y", 2, 2, 0, 3), ("y", 2, 2, 1, 3), ("y", 0, 2, 0, 3), ("y", 3, 2, 0, 3), ("y", 3, 2, 1, 4),
+    ("y", 1, 2, 0, 3), ("y", 2, 2, 0, 4), ("y", 1, 2, 1, 4), ("fin", 1), ("fin", 3), ("fin", 2), ("fin", 4),
+    ("y", 0, 2, 1, 3), ("y", 0, 2, 0, 4), ("fin", 0),
 )
 
 

time: 88.6 us -> 88.1 us (level)
  no operation moved by 1% of the time
where the time goes in v5:
time: 88.1 us; the launch traced here: 88 us
  Pallas kernels  86.3 us (98%)
  local copies, waits for them, and re-layouts  1.61 us (2%)
    pallas_call x1, Pallas kernels, body(): pl.pallas_call(kernel, out_shape=jax.ShapeDtypeStruct((ROWS, WIDTH), F32)...  86.3 us

profile of v5, /device:TPU:6, one launch (start us, length us, event | category | flops | bytes accessed | tf_op | source)
XLA Modules:
  0.0 88.0 jit_solution(10283348810128289350)
XLA Ops:
  0.0 86.3 %shard_map.46 = f32[72,576]{1,0:T(8,128)} custom-call(bf16[72,576]{1,0:T(8,128)(2,1)} %x_hbm.1, bf16[72,576]{1,0:T(8,128)(2,1)} %t_hbm.1, s32[36,36]{1,0:T(8,128)} %fx_hbm.1, s32[36,36]{1,0:T(8,128)} %ft_hbm.1), custom_call_target="tpu_custom_call" | custom-call | tf_op jit(solution)/shard_map/pallas_call | solution.py:408
  86.4 1.6 %copy.6 = f32[72,576]{1,0:T(8,128)} copy(f32[72,576]{1,0:T(8,128)} %shard_map.46) | data formatting | bytes 331776
